TPU v7x, 32 devices: a whole 2x2x4 slice. The times are simulated.
32 devices in a mesh: groups: 2 (over x), seq: 16 (over z, y, core).
Axes of the slice: x: 2, y: 2, z: 4, core: 2. Of those that a mesh axis runs over, the one named last changes fastest.
Arguments:
- frame_queries: bfloat16 [4096, 768], P(('groups', 'seq')), parts along dimension 0, may hold values from -8 to 8
- frame_keys: bfloat16 [4096, 768], P(('groups', 'seq')), parts along dimension 0, may hold values from -8 to 8
- frame_values: bfloat16 [4096, 768], P(('groups', 'seq')), parts along dimension 0, may hold values from -6 to 6
- cotangent: bfloat16 [4096, 768], P(('groups', 'seq')), parts along dimension 0, may hold values from -6 to 6
- frame_mask: int32 [4096], P(('groups', 'seq')), parts along dimension 0, may hold values from 0 to 1, as said below
- global_rows: int32 [256], P('groups'), parts along dimension 0, may hold values from 0 to 1023, as said below
- position_bias: float32 [12, 255], replicated, may hold values from -4 to 4
Outputs:
- attended: bfloat16 [4096, 768], P(('groups', 'seq')), parts along dimension 0
- grad_queries: bfloat16 [4096, 768], P(('groups', 'seq')), parts along dimension 0
- grad_keys: bfloat16 [4096, 768], P(('groups', 'seq')), parts along dimension 0
- grad_values: bfloat16 [4096, 768], P(('groups', 'seq')), parts along dimension 0
- grad_bias: float32 [24, 255], P('groups'), parts along dimension 0
There are 2 independent parts, one for each index of `groups`. A program takes and returns all parts, laid end to end along the dimension named above; an argument that names none is the same for every part. Nothing has to cross between parts.
Inputs may be any that keep to these rules, and one draw needn't show every extreme that they name: `frame_mask`: ones on a prefix of more than 1024 frames and zeros after it; at least one zero. `global_rows`: 128 distinct frame indices below 1024, so all on live frames; 0 and 1023 both occur.
All inputs are finite; a program needn't handle non-finite values.
Results may differ from a plain program's by a relative error of at most 0.008.
The roundings to bfloat16 on the way count: a program that leaves them out, or rounds other values in their place, can miss the bound.
Values may be sent and summed in bfloat16 or wider, within the bound.
No kernel may reach another device: no remote copies, remote signals or barrier semaphores. Data moves between devices by JAX's collectives and lax.ppermute only.
A program may use at most 64 MiB of HBM per device.

v0:
```python
import jax
import jax.numpy as jnp
from jax import lax
from jax.sharding import PartitionSpec as P

NEG_BIG = -1e30


def padded_2(cells, sides, width):
    for axis, dim in sides:
        count = lax.axis_size(axis)
        ends = count - 1
        head = lax.slice_in_dim(cells, 0, width, axis=dim)
        tail = lax.slice_in_dim(cells, cells.shape[dim] - width, cells.shape[dim], axis=dim)
        cells = jnp.concatenate(
            [
                lax.ppermute(tail, axis, [(i, (i + 1) % count) for i in range(ends)]),
                cells,
                lax.ppermute(head, axis, [((i + 1) % count, i) for i in range(ends)]),
            ],
            axis=dim,
        )
    return cells


def bias_block(position_bias, band_rows):
    head_count, span_len = position_bias.shape
    tiled = jnp.broadcast_to(position_bias[:, None, :], (head_count, band_rows, span_len))
    tiled = jnp.pad(tiled.reshape(head_count, band_rows * span_len), ((0, 0), (0, band_rows)))
    shifted = tiled.reshape(head_count, band_rows, span_len + 1)[:, :, : 3 * band_rows]
    return shifted[:, ::-1, :]


def bias_gradient(grad_band, band_rows):
    head_count = grad_band.shape[0]
    span_len = 4 * band_rows - 1
    flipped = grad_band[:, ::-1, :]
    padded = jnp.pad(flipped, ((0, 0), (0, 0), (0, band_rows)))
    flat_rows = padded.reshape(head_count, band_rows * 4 * band_rows)[:, : band_rows * span_len]
    return flat_rows.reshape(head_count, band_rows, span_len).sum(axis=1)


def local(
    frame_queries, frame_keys, frame_values, cotangent, frame_mask, global_rows, position_bias
):
    frames, att_width = frame_queries.shape
    head_count = position_bias.shape[0]
    size_head = att_width // head_count
    band_rows = (position_bias.shape[1] + 1) // 4
    memory = global_rows.shape[0]
    blocks = frames // band_rows
    window = 3 * band_rows
    factor = size_head ** (-0.5)
    anchor = lax.axis_index("seq") * frames
    local_rows = global_rows - anchor
    in_shard = (local_rows >= 0) & (local_rows < frames)
    safe_rows = jnp.clip(local_rows, 0, frames - 1)
    drop_rows = jnp.where(in_shard, local_rows, frames)
    stacked = jnp.concatenate([frame_queries, frame_keys, frame_values, cotangent], axis=1)
    picked_own = jnp.where(
        in_shard[:, None], stacked[safe_rows], jnp.zeros((), jnp.bfloat16)
    ).astype(jnp.float32)
    valid_count = jnp.sum(frame_mask).astype(jnp.float32)
    picked, length = lax.psum((picked_own, valid_count), "seq")
    picked = picked.astype(jnp.bfloat16)
    memory_query = picked[:, :att_width].reshape(memory, head_count, size_head)
    memory_key = picked[:, att_width : 2 * att_width].reshape(memory, head_count, size_head)
    memory_value = picked[:, 2 * att_width : 3 * att_width].reshape(memory, head_count, size_head)
    memory_grad = picked[:, 3 * att_width :].reshape(memory, head_count, size_head)
    key_value = jnp.concatenate([frame_keys, frame_values], axis=1)
    extended = padded_2(key_value, (("seq", 0),), band_rows)
    positions = (anchor - band_rows + lax.iota(jnp.int32, frames + 2 * band_rows)).astype(
        jnp.float32
    )
    usable = (positions >= 0.0) & (positions < length)
    ext_blocks = extended.reshape(blocks + 2, band_rows, 2 * att_width)
    windows = jnp.concatenate([ext_blocks[:-2], ext_blocks[1:-1], ext_blocks[2:]], axis=1)
    usable_blocks = usable.reshape(blocks + 2, band_rows)
    usable_win = jnp.concatenate(
        [usable_blocks[:-2], usable_blocks[1:-1], usable_blocks[2:]], axis=1
    )
    win_keys = windows[:, :, :att_width].reshape(blocks, window, head_count, size_head)
    win_values = windows[:, :, att_width:].reshape(blocks, window, head_count, size_head)
    query_blocks = frame_queries.reshape(blocks, band_rows, head_count, size_head)
    band_scores = (
        jnp.einsum("bihs,bjhs->bhij", query_blocks, win_keys, preferred_element_type=jnp.float32)
        * factor
    )
    band_scores = band_scores + bias_block(position_bias, band_rows)[None]
    band_scores = jnp.where(usable_win[:, None, None, :], band_scores, NEG_BIG)
    memory_scores = (
        jnp.einsum("bihs,ghs->bhig", query_blocks, memory_key, preferred_element_type=jnp.float32)
        * factor
    )
    scores = jnp.concatenate([band_scores, memory_scores], axis=3)
    row_top = jnp.max(scores, axis=3, keepdims=True)
    raised = jnp.exp(scores - row_top)
    band_probs = raised / jnp.sum(raised, axis=3, keepdims=True)
    probs_low = band_probs.astype(jnp.bfloat16)
    band_out = jnp.einsum(
        "bhij,bjhs->bihs", probs_low[..., :window], win_values, preferred_element_type=jnp.float32
    ) + jnp.einsum(
        "bhig,ghs->bihs", probs_low[..., window:], memory_value, preferred_element_type=jnp.float32
    )
    band_out = band_out.astype(jnp.bfloat16).reshape(frames, att_width)
    own_usable = (anchor + lax.iota(jnp.int32, frames)).astype(jnp.float32) < length
    key_heads = frame_keys.reshape(frames, head_count, size_head)
    value_heads = frame_values.reshape(frames, head_count, size_head)
    wide_scores = (
        jnp.einsum("ghs,fhs->ghf", memory_query, key_heads, preferred_element_type=jnp.float32)
        * factor
    )
    wide_scores = jnp.where(own_usable[None, None, :], wide_scores, NEG_BIG)
    local_top = jnp.max(wide_scores, axis=2)
    values_wide = frame_values.astype(jnp.float32).reshape(frames, head_count, size_head)
    wide_top = lax.pmax(local_top, "seq")
    weights = jnp.where(own_usable[None, None, :], jnp.exp(wide_scores - wide_top[..., None]), 0.0)
    total_local = jnp.sum(weights, axis=2)
    numer_local = jnp.einsum(
        "ghf,fhs->ghs", weights, values_wide, precision=lax.Precision.HIGHEST
    ).reshape(memory, att_width)
    wide_total, numerator = lax.psum((total_local, numer_local), "seq")
    memory_out = (numerator.reshape(memory, head_count, size_head) / wide_total[..., None]).astype(
        jnp.bfloat16
    )
    is_memory = jnp.zeros((frames,), jnp.bool_).at[drop_rows].set(True, mode="drop")
    placed = (
        jnp.zeros((frames, att_width), jnp.bfloat16)
        .at[drop_rows]
        .set(memory_out.reshape(memory, att_width), mode="drop")
    )
    live_rows = frame_mask == 1
    attended = jnp.where(is_memory[:, None], placed, band_out)
    attended = jnp.where(live_rows[:, None], attended, jnp.zeros_like(attended))
    keep_rows = live_rows & jnp.logical_not(is_memory)
    grad_in = jnp.where(keep_rows[:, None], cotangent, jnp.zeros_like(cotangent))
    grad_blocks = grad_in.reshape(blocks, band_rows, head_count, size_head)
    row_dot = jnp.sum(
        (grad_in.astype(jnp.float32) * band_out.astype(jnp.float32)).reshape(
            blocks, band_rows, head_count, size_head
        ),
        axis=3,
    )
    row_dot = row_dot.transpose(0, 2, 1)
    grad_probs = jnp.concatenate(
        [
            jnp.einsum(
                "bihs,bjhs->bhij", grad_blocks, win_values, preferred_element_type=jnp.float32
            ),
            jnp.einsum(
                "bihs,ghs->bhig", grad_blocks, memory_value, preferred_element_type=jnp.float32
            ),
        ],
        axis=3,
    )
    grad_scores = band_probs * (grad_probs - row_dot[..., None])
    grad_low = grad_scores.astype(jnp.bfloat16)
    bias_local = bias_gradient(jnp.sum(grad_scores[..., :window], axis=0), band_rows)
    dq_band = factor * (
        jnp.einsum(
            "bhij,bjhs->bihs", grad_low[..., :window], win_keys, preferred_element_type=jnp.float32
        )
        + jnp.einsum(
            "bhig,ghs->bihs", grad_low[..., window:], memory_key, preferred_element_type=jnp.float32
        )
    )
    win_dk = factor * jnp.einsum(
        "bhij,bihs->bjhs", grad_low[..., :window], query_blocks, preferred_element_type=jnp.float32
    )
    win_dv = jnp.einsum(
        "bhij,bihs->bjhs", probs_low[..., :window], grad_blocks, preferred_element_type=jnp.float32
    )
    memory_dk = factor * jnp.einsum(
        "bhig,bihs->ghs", grad_low[..., window:], query_blocks, preferred_element_type=jnp.float32
    )
    memory_dv = jnp.einsum(
        "bhig,bihs->ghs", probs_low[..., window:], grad_blocks, preferred_element_type=jnp.float32
    )
    win_grads = jnp.concatenate(
        [win_dk.reshape(blocks, window, att_width), win_dv.reshape(blocks, window, att_width)],
        axis=2,
    )
    thirds = win_grads.reshape(blocks, 3, band_rows, 2 * att_width)
    spread = (
        jnp.pad(thirds[:, 0], ((0, 2), (0, 0), (0, 0)))
        + jnp.pad(thirds[:, 1], ((1, 1), (0, 0), (0, 0)))
        + jnp.pad(thirds[:, 2], ((2, 0), (0, 0), (0, 0)))
    ).reshape((blocks + 2) * band_rows, 2 * att_width)
    rim_rows = jnp.concatenate([spread[:band_rows], spread[-band_rows:]], axis=0)
    returned = padded_2(rim_rows, (("seq", 0),), band_rows)
    interior = spread[band_rows:-band_rows]
    interior = interior.at[:band_rows].add(returned[:band_rows])
    interior = interior.at[-band_rows:].add(returned[-band_rows:])
    weights_full = jnp.where(
        own_usable[None, None, :], jnp.exp(wide_scores - wide_top[..., None]), 0.0
    )
    shares = weights_full / wide_total[..., None]
    shares_low = shares.astype(jnp.bfloat16)
    grad_wide = jnp.einsum(
        "ghs,fhs->ghf", memory_grad, value_heads, preferred_element_type=jnp.float32
    )
    memory_dot = jnp.sum(memory_grad.astype(jnp.float32) * memory_out.astype(jnp.float32), axis=2)
    grad_wide_low = (shares * (grad_wide - memory_dot[..., None])).astype(jnp.bfloat16)
    dq_memory = factor * jnp.einsum(
        "ghf,fhs->ghs", grad_wide_low, key_heads, preferred_element_type=jnp.float32
    )
    dk_wide = factor * jnp.einsum(
        "ghf,ghs->fhs", grad_wide_low, memory_query, preferred_element_type=jnp.float32
    )
    dv_wide = jnp.einsum(
        "ghf,ghs->fhs", shares_low, memory_grad, preferred_element_type=jnp.float32
    )
    memory_kv = jnp.concatenate(
        [memory_dk.reshape(memory, att_width), memory_dv.reshape(memory, att_width)], axis=1
    )
    summed_kv, summed_q, grad_bias = lax.psum(
        (memory_kv, dq_memory.reshape(memory, att_width), bias_local), "seq"
    )
    back_kv = (
        jnp.zeros((frames, 2 * att_width), jnp.float32).at[drop_rows].add(summed_kv, mode="drop")
    )
    back_q = jnp.zeros((frames, att_width), jnp.float32).at[drop_rows].add(summed_q, mode="drop")
    grad_queries = (dq_band.reshape(frames, att_width) + back_q).astype(jnp.bfloat16)
    grad_keys = (
        interior[:, :att_width] + dk_wide.reshape(frames, att_width) + back_kv[:, :att_width]
    ).astype(jnp.bfloat16)
    grad_values = (
        interior[:, att_width:] + dv_wide.reshape(frames, att_width) + back_kv[:, att_width:]
    ).astype(jnp.bfloat16)
    return (attended, grad_queries, grad_keys, grad_values, grad_bias)


def solution(mesh):
    return jax.shard_map(
        local,
        mesh=mesh,
        in_specs=(
            P(("groups", "seq"), None),
            P(("groups", "seq"), None),
            P(("groups", "seq"), None),
            P(("groups", "seq"), None),
            P(("groups", "seq")),
            P("groups"),
            P(),
        ),
        out_specs=(
            P(("groups", "seq"), None),
            P(("groups", "seq"), None),
            P(("groups", "seq"), None),
            P(("groups", "seq"), None),
            P("groups", None),
        ),
        check_vma=False,
    )
```

profile of v0, /device:TPU:0, one launch (start us, length us, event | category | flops | bytes accessed | tf_op | source)
XLA Modules:
  0.0 375.7 jit_solution(838769824504938073)
XLA Ops:
  10.1 3.0 collective-permute-start
  17.9 77.0 %all-reduce.15 = (bf16[128,3072]{1,0:T(8,128)(2,1)}, f32[]{:T(128)}) all-reduce(f32[128,3072]{1,0:T(8,128)S(1)} %select_convert_fusion, f32[]{:T(128)S(6)} %convert_element_type.76), channel_id=1, replica_groups=mesh['groups'=2,'seq'=16] {'seq'}, use_global_device_ids=true, to_apply=%region_3.4 | all-reduce | flops 393217 | bytes 2359304 | tf_op jit(solution)/shard_map/psum | solution.py:64
  94.9 2.0 fusion.65
  98.2 30.0 %pmax.7 = f32[128,12]{0,1:T(8,128)S(1)} all-reduce(f32[128,12]{0,1:T(8,128)S(1)} %get-tuple-element.63), channel_id=1, replica_groups=mesh['groups'=2,'seq'=16] {'seq'}, use_global_device_ids=true, to_apply=%region_5.6 | all-reduce | flops 1536 | bytes 12288 | tf_op jit(solution)/shard_map/pmax | solution.py:116
  140.1 1.8 pad_maximum_fusion.5
  150.8 2.2 copy.205
  153.0 2.1 reshape.264
  155.1 2.0 convert_multiply_fusion
  157.0 1.7 copy.166
  158.8 1.9 reshape.197
  160.7 2.6 convolution_bitcast_fusion
  166.1 4.3 %reshape.263 = f32[2,3,64,768]{2,1,3,0:T(4,128)} reshape(f32[2,192,12,64]{1,3,2,0:T(8,128)} %convolution_bitcast_fusion) | data formatting | bytes 2359296 | tf_op jit(solution)/shard_map/concatenate | solution.py:179
  170.4 4.1 %copy.184 = f32[2,3,64,768]{3,2,0,1:T(8,128)} copy(f32[2,3,64,768]{2,1,3,0:T(4,128)} %reshape.263) | data formatting | bytes 2359296 | tf_op jit(solution)/shard_map/concatenate | solution.py:179
  175.4 4.2 %fusion.62 = (bf16[2,12,64,320]{3,2,1,0:T(8,128)(2,1)S(1)}, f32[2,12,64,320]{3,2,1,0:T(8,128)}) fusion(f32[2,12,64]{2,1,0:T(8,128)S(1)} %copy.171, f32[2,12,64,128]{3,2,1,0:T(8,128)} %convolution_bitcast_fusion.5, f32[2,12,64,192]{3,2,1,0:T(8,128)} %fusion.46, f32[2,12,64]{2,1,0:T(8,128)} %copy-done.45, f32[2,12,64]{2,1,0:T(8,128)S(1)} %reduce_max.32, ...), kind=kLoop, calls=%fused_computation.124 | loop fusion | flops 3440640 | bytes 6899712 | tf_op jit(solution)/shard_map/convert_element_type | solution.py:157
  182.2 2.9 reshape.262
  185.2 2.2 copy.183
  187.4 1.8 fusion.18
  190.8 2.5 fusion.33
  195.6 57.7 %all-reduce.5 = (f32[128,12]{0,1:T(8,128)S(1)}, f32[12,255]{1,0:T(8,128)}) all-reduce(f32[128,12]{0,1:T(8,128)S(1)} %copy-done.49, f32[12,255]{1,0:T(8,128)S(1)} %reduce_sum.69), channel_id=1, replica_groups=mesh['groups'=2,'seq'=16] {'seq'}, use_global_device_ids=true, to_apply=%region_8.9 | all-reduce | flops 4596 | bytes 36768 | tf_op jit(solution)/shard_map/psum | solution.py:122
  258.5 2.1 collective-permute-start.2
  270.5 1.8 scatter_custom_fusion.1
  275.4 87.2 %all-reduce.14.cloned.1.call-done = (f32[128,768]{1,0:T(8,128)}, f32[128,1536]{1,0:T(8,128)}) async-done(((f32[128,768]{1,0:T(8,128)}, f32[128,1536]{1,0:T(8,128)}), (f32[128,768]{1,0:T(8,128)}, f32[128,1536]{1,0:T(8,128)})) %all-reduce.14.cloned.1.call-update) | async-done | bytes 1179664 | tf_op jit(solution)/shard_map/psum | solution.py:216
  362.6 2.6 scatter_custom_fusion.3
  365.2 2.1 scatter_fusion
  (223 shorter events, 58.0 us)
Async XLA Ops:
  7.2 7.3 %copy-start.19 = (bf16[128,768]{1,0:T(8,128)(2,1)S(1)}, bf16[128,768]{1,0:T(8,128)(2,1)}, u32[]{:S(2)}) copy-start(bf16[128,768]{1,0:T(8,128)(2,1)} %param.12) | copy-start | bytes 589828
  7.2 7.5 %copy-start.18 = (bf16[128,768]{1,0:T(8,128)(2,1)S(1)}, bf16[128,768]{1,0:T(8,128)(2,1)}, u32[]{:S(2)}) copy-start(bf16[128,768]{1,0:T(8,128)(2,1)} %param.13) | copy-start | bytes 589828
  7.2 7.2 %copy-start.58 = (s32[128]{0:T(128)S(1)}, s32[128]{0:T(128)}, u32[]{:S(2)}) copy-start(s32[128]{0:T(128)} %param.16) | copy-start | bytes 1540
  7.2 7.6 %copy-start.36 = (bf16[128,768]{1,0:T(8,128)(2,1)S(1)}, bf16[128,768]{1,0:T(8,128)(2,1)}, u32[]{:S(2)}) copy-start(bf16[128,768]{1,0:T(8,128)(2,1)} %param.11) | copy-start | bytes 589828
  7.2 7.6 %copy-start.35 = (bf16[128,768]{1,0:T(8,128)(2,1)S(1)}, bf16[128,768]{1,0:T(8,128)(2,1)}, u32[]{:S(2)}) copy-start(bf16[128,768]{1,0:T(8,128)(2,1)} %param.14) | copy-start | bytes 589828
  7.2 248.5 %all-reduce.12.cloned.1.call-start = ((), (), s32[]{:S(2)}) async-start(), calls=%async_computation | async-start | bytes 786432 | tf_op jit(solution)/shard_map/psum | solution.py:122
  10.1 130.0 %collective-permute-start = (bf16[64,1536]{1,0:T(8,128)(2,1)}, bf16[64,1536]{1,0:T(8,128)(2,1)}, u32[]{:S(2)}, u32[]{:S(2)}) collective-permute-start(bf16[64,1536]{1,0:T(8,128)(2,1)} %get-tuple-element.54), channel_id=1, source_target_pairs={{0,1},{1,2},{2,3},{3,4},{4,5},{5,6},{6,7},{7,8},{8,9},{9,10},{10,1... | collective-permute-start | bytes 589832 | tf_op jit(solution)/shard_map/ppermute | solution.py:17
  13.1 126.9 %collective-permute-start.1 = (bf16[64,1536]{1,0:T(8,128)(2,1)}, bf16[64,1536]{1,0:T(8,128)(2,1)}, u32[]{:S(2)}, u32[]{:S(2)}) collective-permute-start(bf16[64,1536]{1,0:T(8,128)(2,1)} %get-tuple-element.55), channel_id=1, source_target_pairs={{1,0},{2,1},{3,2},{4,3},{5,4},{6,5},{7,6},{8,7},{9,8},{10,9},{11,1... | collective-permute-start | bytes 589832 | tf_op jit(solution)/shard_map/ppermute | solution.py:19
  14.4 124.0 %copy-start.56 = (s32[128]{0:T(128)}, s32[128]{0:T(128)S(1)}, u32[]{:S(2)}) copy-start(s32[128]{0:T(128)S(1)} %get-tuple-element.62) | copy-start | bytes 1540
  14.6 83.2 %copy-start.21 = (bf16[128,768]{0,1:T(8,128)(2,1)}, bf16[128,768]{0,1:T(8,128)(2,1)S(1)}, u32[]{:S(2)}) copy-start(bf16[128,768]{0,1:T(8,128)(2,1)S(1)} %copy.150) | copy-start | bytes 589828
  14.8 113.4 %copy-start.37 = (bf16[128,768]{0,1:T(8,128)(2,1)}, bf16[128,768]{0,1:T(8,128)(2,1)S(1)}, u32[]{:S(2)}) copy-start(bf16[128,768]{0,1:T(8,128)(2,1)S(1)} %copy.151) | copy-start | bytes 589828
  97.6 32.4 %copy-start.51 = (pred[128]{0:T(512)(128)(4,1)}, pred[128]{0:T(512)(128)(4,1)S(1)}, u32[]{:S(2)}) copy-start(pred[128]{0:T(512)(128)(4,1)S(1)} %convert_compare_fusion.2) | copy-start | bytes 388
  97.8 32.0 %copy-start.23 = (bf16[128,768]{0,1:T(8,128)(2,1)}, bf16[128,768]{0,1:T(8,128)(2,1)S(1)}, u32[]{:S(2)}) copy-start(bf16[128,768]{0,1:T(8,128)(2,1)S(1)} %copy.149) | copy-start | bytes 589828
  98.2 32.6 %copy-start.5 = (f32[128,12,128]{0,2,1:T(8,128)}, f32[128,12,128]{0,2,1:T(8,128)S(1)}, u32[]{:S(2)}) copy-start(f32[128,12,128]{0,2,1:T(8,128)S(1)} %get-tuple-element.64) | copy-start | bytes 2359300
  129.8 232.8 %all-reduce.14.cloned.1.call-start = ((), (), s32[]{:S(2)}) async-start(), calls=%async_computation.1 | async-start | bytes 2359296 | tf_op jit(solution)/shard_map/psum | solution.py:216
  132.8 11.7 %copy-start.12 = (bf16[2,64,12,64]{1,0,3,2:T(2,128)(2,1)}, bf16[2,64,12,64]{1,0,3,2:T(2,128)(2,1)S(1)}, u32[]{:S(2)}) copy-start(bf16[2,64,12,64]{1,0,3,2:T(2,128)(2,1)S(1)} %reshape.191) | copy-start | bytes 589828
  149.1 11.5 %copy-start = (bf16[2,12,64,320]{3,2,1,0:T(8,128)(2,1)}, bf16[2,12,64,320]{3,2,1,0:T(8,128)(2,1)S(1)}, u32[]{:S(2)}) copy-start(bf16[2,12,64,320]{3,2,1,0:T(8,128)(2,1)S(1)} %fusion.52) | copy-start | bytes 2949124
  194.4 59.0 %copy-start.6 = (f32[128,12,128]{0,2,1:T(8,128)S(1)}, f32[128,12,128]{0,2,1:T(8,128)}, u32[]{:S(2)}) copy-start(f32[128,12,128]{0,2,1:T(8,128)} %copy-done.5) | copy-start | bytes 2359300
  194.4 58.9 %copy-start.41 = (bf16[128,768]{0,1:T(8,128)(2,1)S(1)}, bf16[128,768]{0,1:T(8,128)(2,1)}, u32[]{:S(2)}) copy-start(bf16[128,768]{0,1:T(8,128)(2,1)} %copy.173) | copy-start | bytes 589828
  194.4 58.9 %copy-start.47 = (f32[128,12]{0,1:T(8,128)S(1)}, f32[128,12]{0,1:T(8,128)}, u32[]{:S(2)}) copy-start(f32[128,12]{0,1:T(8,128)} %copy-done.46) | copy-start | bytes 18436
  194.4 58.9 %copy-start.52 = (pred[128]{0:T(512)(128)(4,1)S(1)}, pred[128]{0:T(512)(128)(4,1)}, u32[]{:S(2)}) copy-start(pred[128]{0:T(512)(128)(4,1)} %copy-done.51) | copy-start | bytes 388
  258.3 6.6 %copy-start.43 = (f32[12,128,64]{1,2,0:T(8,128)S(1)}, f32[12,128,64]{1,2,0:T(8,128)}, u32[]{:S(2)}) copy-start(f32[12,128,64]{1,2,0:T(8,128)} %fusion.14) | copy-start | bytes 1179652
  258.5 14.7 %collective-permute-start.2 = (f32[64,1536]{1,0:T(8,128)}, f32[64,1536]{1,0:T(8,128)}, u32[]{:S(2)}, u32[]{:S(2)}) collective-permute-start(f32[64,1536]{1,0:T(8,128)} %get-tuple-element.45), channel_id=1, source_target_pairs={{0,1},{1,2},{2,3},{3,4},{4,5},{5,6},{6,7},{7,8},{8,9},{9,10},{10,1... | collective-permute-start | bytes 1179656 | tf_op jit(solution)/shard_map/ppermute | solution.py:17
  260.6 13.7 %collective-permute-start.3 = (f32[64,1536]{1,0:T(8,128)}, f32[64,1536]{1,0:T(8,128)}, u32[]{:S(2)}, u32[]{:S(2)}) collective-permute-start(f32[64,1536]{1,0:T(8,128)} %get-tuple-element.44), channel_id=1, source_target_pairs={{1,0},{2,1},{3,2},{4,3},{5,4},{6,5},{7,6},{8,7},{9,8},{10,9},{11,1... | collective-permute-start | bytes 1179656 | tf_op jit(solution)/shard_map/ppermute | solution.py:19
  (43 other events, 96.3 us)
Sparse Core Ops, SparseCore 0:
  129.9 87.6 all-reduce.11
  270.6 91.9 all-reduce.13
where the time goes:
time: 377 us; the launch traced here: 376 us
  blocking collectives  165 us (44%)
  waiting for transfers between devices  87.3 us (23%)
  local copies, waits for them, and re-layouts  52.5 us (14%)
  other arithmetic  30.4 us (8%)
  matrix products  17.1 us (5%)
  between operations  15.7 us (4%)
  starting transfers between devices  7.98 us (2%)
    psum x1, waiting for transfers between devices, local(): lax.psum((memory_kv, dq_memory.reshape(memory, att_width), bias_local), '...  87.2 us
    psum x1, blocking collectives, local(): picked, length = lax.psum((picked_own, valid_count), 'seq')  77 us
    psum x1, blocking collectives, local(): wide_total, numerator = lax.psum((total_local, numer_local), 'seq')  57.7 us
    pmax x1, blocking collectives, local(): wide_top = lax.pmax(local_top, 'seq')  30 us
    concatenate x4, local copies, waits for them, and re-layouts, local(): jnp.concatenate([win_dk.reshape(blocks, window, att_width), win_dv.reshap...  13.6 us
  transfers between devices with their start and end apart: 6, of which 1 were waited for; matrix products, arithmetic and copies ran while one was open for 23% of the time, Pallas kernels for 0%

commit v1 on v0

v1 whole, which is shorter than its diff:
```python
import jax
import jax.numpy as jnp
from jax import lax
from jax.experimental import pallas as pl
from jax.experimental.pallas import tpu as pltpu
from jax.sharding import PartitionSpec as P

NEG_BIG = -1e30
DEAD = 64.0
BIAS_ROWS = 8
BF16 = jnp.bfloat16
F32 = jnp.float32


def mm(a, b):
    return jnp.dot(a, b, preferred_element_type=F32)


def split2(x):
    high = x.astype(BF16)
    return high, (x - high.astype(F32)).astype(BF16)


def iota(shape, dim):
    return lax.broadcasted_iota(jnp.int32, shape, dim)


def swap_halves(x):
    half = x.shape[1] // 2
    return jnp.concatenate([x[:, half:], x[:, :half]], axis=1)


def pack_kernel(mask_ref, q_ref, k_ref, v_ref, g_ref, out_ref):
    slots, rows, _ = out_ref.shape
    pairs = q_ref.shape[1] // 128
    live = jnp.sum(mask_ref[...])
    alive = iota((rows, 128), 0) < live
    low = iota((rows, 128), 1) < 64
    for i in range(pairs):
        at = slice(128 * i, 128 * (i + 1))
        q, k, v = q_ref[:, at], k_ref[:, at], v_ref[:, at]
        g = jnp.where(alive, g_ref[:, at], jnp.asarray(DEAD, BF16))
        out_ref[2 * i, :, 0:128] = jnp.where(low, k, swap_halves(v))
        out_ref[2 * i + 1, :, 0:128] = jnp.where(low, swap_halves(k), v)
        out_ref[2 * i, :, 128:256] = jnp.where(low, q, swap_halves(g))
        out_ref[2 * i + 1, :, 128:256] = jnp.where(low, swap_halves(q), g)

    @pl.loop(2 * pairs, slots)
    def _(s):
        out_ref[s] = jnp.zeros(out_ref.shape[1:], BF16)


def unpack_kernel(in_ref, att_ref, dq_ref, dk_ref, dv_ref, gb_ref):
    rows = att_ref.shape[0]
    pairs = att_ref.shape[1] // 128
    low = iota((rows, 128), 1) < 64
    for i in range(pairs):
        at = slice(128 * i, 128 * (i + 1))
        a, b = in_ref[2 * i, :rows, 0:128], in_ref[2 * i + 1, :rows, 0:128]
        dk_ref[:, at] = jnp.where(low, a, swap_halves(b))
        dv_ref[:, at] = jnp.where(low, swap_halves(a), b)
        a, b = in_ref[2 * i, :rows, 128:256], in_ref[2 * i + 1, :rows, 128:256]
        dq_ref[:, at] = jnp.where(low, a, swap_halves(b))
        att_ref[:, at] = jnp.where(low, swap_halves(a), b)
    for h in range(2 * pairs):
        parts = in_ref[h, rows:, :].astype(F32)
        whole = parts[0:1] + parts[1:2] + parts[2:3]
        gb_ref[h : h + 1, :] = whole[:, : gb_ref.shape[1]]


def shear(x, first, step):
    rows, lanes = x.shape
    row = iota(x.shape, 0)
    x = pltpu.roll(x, first % lanes, 1)
    bit = 1
    while bit < rows:
        x = jnp.where((row & bit) != 0, pltpu.roll(x, (step * bit) % lanes, 1), x)
        bit *= 2
    return x


def core_kernel(
    rows_ref, bias_ref, x_ref, y_ref, kv_ref, kvt_ref, qd_ref, qdt_ref, ww_ref, tb_ref, gb_ref, gm_ref
):
    slots, tile, _ = x_ref.shape
    frames = slots * tile
    blk = tile // 2
    heads, span = bias_ref.shape
    memory = rows_ref.shape[1]
    scale = 64 ** (-0.5)
    owner = lax.axis_index("seq")

    @pl.when(owner < heads)
    def _():
        low_lane = iota((tile, 128), 1) < 64
        low_row = iota((128, 128), 0) < 64
        gr_row = jnp.broadcast_to(rows_ref[...], (128, memory))
        gr_col = gr_row.T
        lane = iota((128, 128), 1)
        sub = iota((128, 128), 0)

        def count(s, c):
            g = x_ref[s, :, 128:256].astype(F32)
            return c + jnp.sum((g < 0.5 * DEAD).astype(F32), axis=0, keepdims=True)

        counts = lax.fori_loop(0, slots, count, jnp.zeros((1, 128), F32))
        length = jnp.max(counts[:, 64:65], axis=1, keepdims=True).astype(jnp.int32)

        def gather(s, c):
            pick = (gr_col == lane + s * tile).astype(BF16)
            return c + mm(pick, x_ref[s])

        mem = lax.fori_loop(0, slots // 2, gather, jnp.zeros((128, 256), F32))
        mkv = mem[:, 0:128].astype(BF16)
        mqo = jnp.where(lane < 64, mem[:, 128:256] * scale, mem[:, 128:256]).astype(BF16)
        mkv_t = mkv.T
        mqo_t = mqo.T

        zeros = jnp.zeros((blk, 128), BF16)
        kv_ref[0:blk, :] = zeros
        kv_ref[frames + blk :, :] = zeros
        ww_ref[0:blk, 0:128] = zeros.astype(F32)
        ww_ref[frames + blk :, 0:128] = zeros.astype(F32)

        def prepare(s, c):
            at = pl.multiple_of(s * tile, tile)
            kv_ref[pl.ds(pl.multiple_of(at + blk, blk), tile), :] = x_ref[s, :, 0:128]
            mine = jnp.max((gr_row == sub + at).astype(F32), axis=1, keepdims=True)
            keep = (mine < 0.5) & (sub[:, 0:1] + at < length)
            qd = x_ref[s, :, 128:256].astype(F32)
            qd = jnp.where(low_lane, qd * scale, jnp.where(keep, qd, 0.0)).astype(BF16)
            qd_ref[pl.ds(at, tile), :] = qd
            qdt_ref[:, pl.ds(at, tile)] = qd.T
            return c

        lax.fori_loop(0, slots, prepare, 0)

        def turn(s, c):
            at = pl.multiple_of(s * tile, tile)
            kvt_ref[:, pl.ds(at, tile)] = kv_ref[pl.ds(at, tile), :].T
            return c

        lax.fori_loop(0, slots + 1, turn, 0)

        head = jnp.minimum(owner, heads - 1)
        b_row = jnp.concatenate([bias_ref[pl.ds(head, 1), :], jnp.zeros((1, 384 - span), F32)], axis=1)
        table = shear(jnp.broadcast_to(b_row, (128, 384)), 1 - blk, 1)[:, : 2 * tile].T
        gap = iota(table.shape, 0) // blk - iota(table.shape, 1) // blk
        tb_ref[...] = jnp.where((gap >= 0) & (gap <= 2), table, NEG_BIG)
        gb_ref[...] = jnp.zeros_like(gb_ref)
        gm_ref[...] = jnp.zeros_like(gm_ref)

        zero_t = jnp.zeros_like(mqo_t)
        wide_rhs = jnp.concatenate(
            [jnp.where(low_row, mqo_t, zero_t), jnp.where(low_row, zero_t, mqo_t)], axis=1
        )
        wide_back = jnp.concatenate(
            [jnp.where(low_lane, mqo, zero_t), jnp.where(low_lane, zero_t, mqo)], axis=0
        )

        def wide_scores(s, top):
            at = pl.multiple_of(s * tile + blk, blk)
            both = mm(kv_ref[pl.ds(at, tile), :], wide_rhs)
            w = jnp.where(sub + s * tile < length, both[:, 0:128], NEG_BIG)
            ww_ref[pl.ds(at, tile), 0:128] = w
            ww_ref[pl.ds(at, tile), 128:256] = both[:, 128:256]
            return jnp.maximum(top, jnp.max(w, axis=0, keepdims=True))

        top = lax.fori_loop(0, slots, wide_scores, jnp.full((1, 128), NEG_BIG, F32))

        def wide_sums(s, c):
            total, numer = c
            at = pl.multiple_of(s * tile + blk, blk)
            e = jnp.exp(ww_ref[pl.ds(at, tile), 0:128] - top)
            e = jnp.where(sub + s * tile < length, e, 0.0)
            ww_ref[pl.ds(at, tile), 0:128] = e
            v_t = x_ref[s, :, 0:128].T[64:128, :]
            high, rest = split2(e)
            numer = numer + mm(v_t, jnp.concatenate([high, rest], axis=1))
            return total + jnp.sum(e, axis=0, keepdims=True), numer

        total, numer = lax.fori_loop(
            0, slots, wide_sums, (jnp.zeros((1, 128), F32), jnp.zeros((64, 256), F32))
        )
        mem_out = ((numer[:, 0:128] + numer[:, 128:256]) / total).astype(BF16)
        mem_dot = jnp.sum(mqo_t[64:128].astype(F32) * mem_out.astype(F32), axis=0, keepdims=True)
        share = 1.0 / total

        def wide_grads(s, dq):
            at = pl.multiple_of(s * tile + blk, blk)
            p = ww_ref[pl.ds(at, tile), 0:128] * share
            dw = (p * (ww_ref[pl.ds(at, tile), 128:256] - mem_dot)).astype(BF16)
            k_t = x_ref[s, :, 0:128].T[0:64, :]
            ww_ref[pl.ds(at, tile), 0:128] = mm(
                jnp.concatenate([dw, p.astype(BF16)], axis=1), wide_back
            )
            return dq + mm(k_t, dw)

        mem_dq = lax.fori_loop(0, slots, wide_grads, jnp.zeros((64, 128), F32)) * scale
        dq_high, dq_rest = split2(mem_dq)
        mem_rows = jnp.concatenate([dq_high, mem_out, dq_rest, jnp.zeros_like(mem_out)], axis=0)

        def band(s, c):
            at = pl.multiple_of(s * tile, tile)
            win = pl.ds(at, 2 * tile)
            qd, qd_t = qd_ref[pl.ds(at, tile), :], qdt_ref[:, pl.ds(at, tile)]
            rhs = jnp.concatenate(
                [jnp.where(low_row, qd_t, zero_t), jnp.where(low_row, zero_t, qd_t)], axis=1
            )
            back = jnp.concatenate(
                [jnp.where(low_lane, qd, zero_t), jnp.where(low_lane, zero_t, qd)], axis=0
            )
            near, far = mm(kv_ref[win, :], rhs), mm(mkv, rhs)
            place = iota((2 * tile, 128), 0) + (at - blk)
            s_near = jnp.where(
                (place >= 0) & (place < length), near[:, 0:128] + tb_ref[...], NEG_BIG
            )
            s_far = far[:, 0:128]
            high = jnp.maximum(
                jnp.max(s_near, axis=0, keepdims=True), jnp.max(s_far, axis=0, keepdims=True)
            )
            e_near, e_far = jnp.exp(s_near - high), jnp.exp(s_far - high)
            inv = 1.0 / (
                jnp.sum(e_near, axis=0, keepdims=True) + jnp.sum(e_far, axis=0, keepdims=True)
            )
            p_near, p_far = e_near * inv, e_far * inv
            pb_near, pb_far = p_near.astype(BF16), p_far.astype(BF16)
            out = mm(kvt_ref[64:128, win], pb_near) + mm(mkv_t[64:128], pb_far)
            out = out.astype(BF16).astype(F32)
            row_dot = jnp.sum(qd_t[64:128].astype(F32) * out, axis=0, keepdims=True)
            ds_near = p_near * (near[:, 128:256] - row_dot)
            ds_far = p_far * (far[:, 128:256] - row_dot)
            gb_ref[...] += ds_near
            db_near, db_far = ds_near.astype(BF16), ds_far.astype(BF16)
            dq = mm(kvt_ref[0:64, win], db_near) + mm(mkv_t[0:64], db_far)
            ww_ref[win, 0:128] += mm(jnp.concatenate([db_near, pb_near], axis=1), back)
            gm_ref[...] += mm(jnp.concatenate([db_far, pb_far], axis=1), back)
            pick = (gr_col == lane + at).astype(F32)
            mine = jnp.max(pick, axis=0, keepdims=True)
            placed = mm(mem_rows, pick.astype(BF16))
            live = lane[0:1] + at < length
            out = jnp.where(live, jnp.where(mine > 0.5, placed[64:128], out), 0.0)
            dq = dq * scale + (placed[0:64] + placed[128:192])
            y_ref[s, 0:tile, 128:256] = jnp.concatenate([dq, out], axis=0).astype(BF16).T
            return c

        lax.fori_loop(0, slots, band, 0)

        mem_back = jnp.concatenate(split2(gm_ref[...]), axis=0)

        wide_bias = jnp.concatenate([gb_ref[...], jnp.zeros((128, 128), F32)], axis=0).T
        bias_sum = jnp.sum(shear(wide_bias, blk - 1, -1), axis=0, keepdims=True)[:, 0:256]
        b0 = bias_sum.astype(BF16).astype(F32)
        b1 = (bias_sum - b0).astype(BF16).astype(F32)
        b2 = bias_sum - b0 - b1
        bias_rows = jnp.concatenate(
            [b0, b1, b2, jnp.zeros((BIAS_ROWS - 3, 256), F32)], axis=0
        ).astype(BF16)

        def finish(s, c):
            at = pl.multiple_of(s * tile, tile)
            pick = (gr_row == sub + at).astype(BF16)
            grads = ww_ref[pl.ds(pl.multiple_of(at + blk, blk), tile), 0:128] + mm(
                jnp.concatenate([pick, pick], axis=1), mem_back
            )
            y_ref[s, 0:tile, 0:128] = grads.astype(BF16)
            y_ref[s, tile:, :] = bias_rows
            return c

        lax.fori_loop(0, slots, finish, 0)


def vmem(shape, dtype):
    return pltpu.VMEM(shape, dtype)


def local(
    frame_queries, frame_keys, frame_values, cotangent, frame_mask, global_rows, position_bias
):
    slots = lax.axis_size("seq")
    tile, width = frame_queries.shape
    heads, span = position_bias.shape
    memory = global_rows.shape[0]
    frames = slots * tile
    wide = pltpu.CompilerParams(vmem_limit_bytes=60 * 1024 * 1024)

    packed = pl.pallas_call(
        pack_kernel,
        out_shape=jax.ShapeDtypeStruct((slots, tile, 256), BF16),
        compiler_params=wide,
    )(frame_mask.reshape(1, tile), frame_queries, frame_keys, frame_values, cotangent)
    by_head = lax.all_to_all(packed, "seq", 0, 0, tiled=True)
    grads = pl.pallas_call(
        core_kernel,
        out_shape=jax.ShapeDtypeStruct((slots, tile + BIAS_ROWS, 256), BF16),
        scratch_shapes=[
            vmem((frames + tile, 128), BF16),
            vmem((128, frames + tile), BF16),
            vmem((frames, 128), BF16),
            vmem((128, frames), BF16),
            vmem((frames + tile, 256), F32),
            vmem((2 * tile, 128), F32),
            vmem((2 * tile, 128), F32),
            vmem((128, 128), F32),
        ],
        compiler_params=wide,
    )(global_rows.reshape(1, memory), position_bias, by_head)
    by_frame = lax.all_to_all(grads, "seq", 0, 0, tiled=True)
    rows = jax.ShapeDtypeStruct((tile, width), BF16)
    attended, dq, dk, dv, grad_bias = pl.pallas_call(
        unpack_kernel,
        out_shape=(rows, rows, rows, rows, jax.ShapeDtypeStruct((heads, span), F32)),
        compiler_params=wide,
    )(by_frame)
    return (attended, dq, dk, dv, grad_bias)


def solution(mesh):
    return jax.shard_map(
        local,
        mesh=mesh,
        in_specs=(
            P(("groups", "seq"), None),
            P(("groups", "seq"), None),
            P(("groups", "seq"), None),
            P(("groups", "seq"), None),
            P(("groups", "seq")),
            P("groups"),
            P(),
        ),
        out_specs=(
            P(("groups", "seq"), None),
            P(("groups", "seq"), None),
            P(("groups", "seq"), None),
            P(("groups", "seq"), None),
            P("groups", None),
        ),
        check_vma=False,
    )
```

time: 377 us -> 106 us (0.28)
  blocking collectives: 165 us -> 65.5 us
  waiting for transfers between devices: 87.3 us -> 0 us
  local copies, waits for them, and re-layouts: 52.5 us -> 0 us
  Pallas kernels: 0 us -> 39.4 us
  other arithmetic: 30.4 us -> 0 us
  matrix products: 17.1 us -> 0 us
  between operations: 15.7 us -> 0.64 us
  starting transfers between devices: 7.98 us -> 0 us
    psum x2 -> x0, blocking collectives: 135 us -> none  [the longest x1 77 us: local(): picked, length = lax.psum((picked_own, valid_count), 'seq')]
    psum x2 -> x0, waiting for transfers between devices: 87.2 us -> none  [the longest x1 87.2 us: local(): lax.psum((memory_kv, dq_memory.reshape(memory, att_width), bias_local), '...]
    all_to_all x0 -> x2, blocking collectives: none -> 65.5 us  [the longest x1 33.1 us: local(): by_frame = lax.all_to_all(grads, 'seq', 0, 0, tiled=True)]
    pallas_call x0 -> x3, Pallas kernels: none -> 39.4 us  [the longest x1 34.4 us: local(): pl.pallas_call(core_kernel, out_shape=jax.ShapeDtypeStruct((slots, tile +...]
    pmax x1 -> x0, blocking collectives: 30 us -> none  [local(): wide_top = lax.pmax(local_top, 'seq')]
    dot_general x17 -> x0, matrix products: 16.9 us -> none  [the longest x1 2.64 us: local(): jnp.einsum('bhij,bihs->bjhs', probs_low[..., :window], grad_blocks, prefe...]
    reshape x16 -> x0, local copies, waits for them, and re-layouts: 15.1 us -> none  [the longest x2 4.24 us: local(): band_out = band_out.astype(jnp.bfloat16).reshape(frames, att_width)]
    concatenate x5 -> x0, local copies, waits for them, and re-layouts: 14.5 us -> none  [the longest x4 13.6 us: local(): jnp.concatenate([win_dk.reshape(blocks, window, att_width), win_dv.reshap...]
  transfers between devices with their start and end apart: 6 -> 0, of which waited for: 1 -> 0; matrix products, arithmetic and copies ran while one was open for 23% -> 0% of each run, Pallas kernels for 0% -> 0%
where the time goes in v1:
time: 106 us; the launch traced here: 105 us
  blocking collectives  65.5 us (62%)
  Pallas kernels  39.4 us (37%)
    pallas_call x1, Pallas kernels, local(): pl.pallas_call(core_kernel, out_shape=jax.ShapeDtypeStruct((slots, tile +...  34.4 us
    all_to_all x1, blocking collectives, local(): by_frame = lax.all_to_all(grads, 'seq', 0, 0, tiled=True)  33.1 us
    all_to_all x1, blocking collectives, local(): by_head = lax.all_to_all(packed, 'seq', 0, 0, tiled=True)  32.3 us
    pallas_call x1, Pallas kernels, local(): pl.pallas_call(pack_kernel, out_shape=jax.ShapeDtypeStruct((slots, tile,...  2.56 us
    pallas_call x1, Pallas kernels, local(): pl.pallas_call(unpack_kernel, out_shape=(rows, rows, rows, rows, jax.Shap...  2.37 us

profile of v1, /device:TPU:0, one launch (start us, length us, event | category | flops | bytes accessed | tf_op | source)
XLA Modules:
  0.0 105.4 jit_solution(16610806170705906097)
XLA Ops:
  0.6 2.6 %shard_map.110 = bf16[16,128,256]{2,1,0:T(8,128)(2,1)} custom-call(s32[1,128]{1,0:T(1,128)} %bitcast.3, bf16[128,768]{1,0:T(8,128)(2,1)} %q_ref.1, bf16[128,768]{1,0:T(8,128)(2,1)} %k_ref.1, bf16[128,768]{1,0:T(8,128)(2,1)} %v_ref.1, bf16[128,768]{1,0:T(8,128)(2,1)} %g_ref.1), custom_call_target="tpu_custom_call" | custom-call | tf_op jit(solution)/shard_map/pallas_call | solution.py:287
  3.2 32.3 %all_to_all.10.x_ref = bf16[16,128,256]{2,1,0:T(8,128)(2,1)} all-to-all(bf16[16,128,256]{2,1,0:T(8,128)(2,1)} %shard_map.110), channel_id=1, replica_groups=mesh['groups'=2,'seq'=16] {'seq'}, dimensions={0} | all-to-all | bytes 2097152 | tf_op jit(solution)/shard_map/all_to_all | solution.py:292
  35.5 34.4 %shard_map.111 = bf16[16,136,256]{2,1,0:T(8,128)(2,1)} custom-call(s32[1,128]{1,0:T(1,128)} %bitcast.2, f32[12,255]{1,0:T(8,128)} %bias_ref.1, bf16[16,128,256]{2,1,0:T(8,128)(2,1)} %all_to_all.10.x_ref), custom_call_target="tpu_custom_call" | custom-call | tf_op jit(solution)/shard_map/pallas_call | solution.py:293
  70.0 33.1 %all_to_all.11.in_ref = bf16[16,136,256]{2,1,0:T(8,128)(2,1)} all-to-all(bf16[16,136,256]{2,1,0:T(8,128)(2,1)} %shard_map.111), channel_id=1, replica_groups=mesh['groups'=2,'seq'=16] {'seq'}, dimensions={0} | all-to-all | bytes 2228224 | tf_op jit(solution)/shard_map/all_to_all | solution.py:308
  103.1 2.4 %shard_map.112 = (bf16[128,768]{1,0:T(8,128)(2,1)}, bf16[128,768]{1,0:T(8,128)(2,1)}, bf16[128,768]{1,0:T(8,128)(2,1)}, bf16[128,768]{1,0:T(8,128)(2,1)}, f32[12,255]{1,0:T(8,128)}) custom-call(bf16[16,136,256]{2,1,0:T(8,128)(2,1)} %all_to_all.11.in_ref), custom_call_target="tpu_custom_call" | custom-call | tf_op jit(solution)/shard_map/pallas_call | solution.py:310

commit v2 on v1

v2 whole, which is shorter than its diff:
```python
import jax
import jax.numpy as jnp
from jax import lax
from jax.experimental import pallas as pl
from jax.experimental.pallas import tpu as pltpu
from jax.sharding import PartitionSpec as P

NEG_BIG = -1e30
DEAD = 64.0
BIAS_ROWS = 8
GROUP = 8
BAND_GROUP = 16
BF16 = jnp.bfloat16
F32 = jnp.float32


def mm(a, b):
    return jnp.dot(a, b, preferred_element_type=F32)


def split2(x):
    high = x.astype(BF16)
    return high, (x - high.astype(F32)).astype(BF16)


def iota(shape, dim):
    return lax.broadcasted_iota(jnp.int32, shape, dim)


def swap_halves(x):
    half = x.shape[1] // 2
    return jnp.concatenate([x[:, half:], x[:, :half]], axis=1)


def pack_kernel(*refs):
    sources, out_ref, held, sem = refs[:5], refs[5], refs[6:11], refs[11]
    copies = [
        pltpu.make_async_copy(source, here, sem.at[i])
        for i, (source, here) in enumerate(zip(sources, held))
    ]
    for copy in copies:
        copy.start()
    mask_ref, k_ref, v_ref, q_ref, g_ref = held
    slots, rows, _ = out_ref.shape
    pairs = q_ref.shape[1] // 128
    low = iota((rows, 128), 1) < 64

    @pl.loop(2 * pairs, slots)
    def _(s):
        out_ref[s] = jnp.zeros(out_ref.shape[1:], BF16)

    for copy in copies[:3]:
        copy.wait()
    for i in range(pairs):
        at = slice(128 * i, 128 * (i + 1))
        k, v = k_ref[:, at], v_ref[:, at]
        out_ref[2 * i, :, 0:128] = jnp.where(low, k, swap_halves(v))
        out_ref[2 * i + 1, :, 0:128] = jnp.where(low, swap_halves(k), v)
    for copy in copies[3:]:
        copy.wait()
    alive = iota((rows, 128), 0) < jnp.sum(mask_ref[...])
    for i in range(pairs):
        at = slice(128 * i, 128 * (i + 1))
        q, g = q_ref[:, at], jnp.where(alive, g_ref[:, at], jnp.asarray(DEAD, BF16))
        out_ref[2 * i, :, 128:256] = jnp.where(low, q, swap_halves(g))
        out_ref[2 * i + 1, :, 128:256] = jnp.where(low, swap_halves(q), g)


def unpack_kernel(in_ref, att_ref, dq_ref, dk_ref, dv_ref, gb_ref):
    rows = att_ref.shape[0]
    pairs = att_ref.shape[1] // 128
    low = iota((rows, 128), 1) < 64
    for i in range(pairs):
        at = slice(128 * i, 128 * (i + 1))
        a, b = in_ref[2 * i, :rows, 0:128], in_ref[2 * i + 1, :rows, 0:128]
        dk_ref[:, at] = jnp.where(low, a, swap_halves(b))
        dv_ref[:, at] = jnp.where(low, swap_halves(a), b)
        a, b = in_ref[2 * i, :rows, 128:256], in_ref[2 * i + 1, :rows, 128:256]
        dq_ref[:, at] = jnp.where(low, a, swap_halves(b))
        att_ref[:, at] = jnp.where(low, swap_halves(a), b)
    for h in range(2 * pairs):
        parts = in_ref[h, rows:, :].astype(F32)
        whole = parts[0:1] + parts[1:2] + parts[2:3]
        gb_ref[h : h + 1, :] = whole[:, : gb_ref.shape[1]]


def shear(x, first, step):
    rows, lanes = x.shape
    row = iota(x.shape, 0)
    x = pltpu.roll(x, first % lanes, 1)
    bit = 1
    while bit < rows:
        x = jnp.where((row & bit) != 0, pltpu.roll(x, (step * bit) % lanes, 1), x)
        bit *= 2
    return x


def core_kernel(
    rows_ref, bias_ref, x_ref, y_ref, kv_ref, kvt_ref, qd_ref, qdt_ref, ww_ref, tb_ref, gb_ref, gm_ref
):
    slots, tile, _ = x_ref.shape
    frames = slots * tile
    blk = tile // 2
    heads, span = bias_ref.shape
    memory = rows_ref.shape[1]
    scale = 64 ** (-0.5)
    owner = lax.axis_index("seq")
    chunk = GROUP * tile

    @pl.when(owner < heads)
    def _():
        lane = iota((128, 128), 1)
        sub = iota((128, 128), 0)
        low_lane = lane < 64
        low_row = sub < 64
        gr_row = jnp.broadcast_to(rows_ref[...], (128, memory))
        gr_col = gr_row.T
        zero_t = jnp.zeros((128, 128), BF16)

        def side(top, bottom):
            return jnp.concatenate([top, bottom], axis=1)

        def spread(x_t):
            return side(jnp.where(low_row, x_t, zero_t), jnp.where(low_row, zero_t, x_t))

        def stack(x):
            return jnp.concatenate(
                [jnp.where(low_lane, x, zero_t), jnp.where(low_lane, zero_t, x)], axis=0
            )

        def over_rows(body, carry):
            carry = lax.fori_loop(
                0, slots // GROUP, lambda i, c: body(pl.multiple_of(i * chunk, chunk), chunk, c), carry
            )
            return body(frames, tile, carry)

        def usable(at, rows, length):
            place = iota((rows, 128), 0) + (at - blk)
            return (place >= 0) & (place < length)

        zeros = jnp.zeros((blk, 128), BF16)
        kv_ref[0:blk, :] = zeros
        kv_ref[frames + blk :, :] = zeros
        wide_low = iota((chunk, 128), 1) < 64
        wide_sub = iota((chunk, 128), 0)
        wide_lane = iota((128, chunk), 1)
        wide_row = jnp.broadcast_to(gr_row[0:1], (chunk, memory))
        wide_col = jnp.concatenate([gr_col] * GROUP, axis=1)
        ones = jnp.ones((memory, 128), BF16)

        def prepare(first_half):
            def body(i, c):
                count, mem = c
                at = pl.multiple_of(i * chunk, chunk)
                x = x_ref[pl.ds(i * GROUP, GROUP)].reshape(chunk, 256)
                kv_ref[pl.ds(pl.multiple_of(at + blk, blk), chunk), :] = x[:, 0:128]
                qd = x[:, 128:256].astype(F32)
                alive = qd < 0.5 * DEAD
                count = count + jnp.sum(alive.astype(F32), axis=0, keepdims=True)
                keep = alive
                if first_half:
                    mem = mem + mm((wide_col == wide_lane + at).astype(BF16), x)
                    mine = mm((wide_row == wide_sub + at).astype(BF16), ones)
                    keep = alive & (mine < 0.5)
                qd = jnp.where(wide_low, qd * scale, jnp.where(keep, qd, 0.0)).astype(BF16)
                qd_ref[pl.ds(at, chunk), :] = qd
                qdt_ref[:, pl.ds(at, chunk)] = qd.T
                return count, mem

            return body

        steps = slots // GROUP
        carry = (jnp.zeros((1, 128), F32), jnp.zeros((128, 256), F32))
        carry = lax.fori_loop(0, steps // 2, prepare(True), carry)
        count, mem = lax.fori_loop(steps // 2, steps, prepare(False), carry)
        length = jnp.max(count[:, 64:65], axis=1, keepdims=True).astype(jnp.int32)
        mkv = mem[:, 0:128].astype(BF16)
        mqo = jnp.where(low_lane, mem[:, 128:256] * scale, mem[:, 128:256]).astype(BF16)
        mkv_t = mkv.T
        mqo_t = mqo.T

        head = jnp.minimum(owner, heads - 1)
        b_row = side(bias_ref[pl.ds(head, 1), :], jnp.zeros((1, 384 - span), F32))
        table = shear(jnp.broadcast_to(b_row, (128, 384)), 1 - blk, 1)[:, : 2 * tile].T
        gap = iota(table.shape, 0) // blk - iota(table.shape, 1) // blk
        tb_ref[...] = jnp.where((gap >= 0) & (gap <= 2), table, NEG_BIG)
        gb_ref[...] = jnp.zeros_like(gb_ref)
        gm_ref[...] = jnp.zeros_like(gm_ref)

        wide_rhs = spread(mqo_t)
        wide_back = stack(mqo)

        def wide_scores(at, rows, top):
            kv = kv_ref[pl.ds(at, rows), :]
            kvt_ref[:, pl.ds(at, rows)] = kv.T
            both = mm(kv, wide_rhs)
            w = jnp.where(usable(at, rows, length), both[:, 0:128], NEG_BIG)
            ww_ref[pl.ds(at, rows), 0:128] = w
            ww_ref[pl.ds(at, rows), 128:256] = both[:, 128:256]
            return jnp.maximum(top, jnp.max(w, axis=0, keepdims=True))

        top = over_rows(wide_scores, jnp.full((1, 128), NEG_BIG, F32))

        def wide_sums(at, rows, c):
            total, numer = c
            e = jnp.exp(ww_ref[pl.ds(at, rows), 0:128] - top)
            e = jnp.where(usable(at, rows, length), e, 0.0)
            ww_ref[pl.ds(at, rows), 0:128] = e
            high, rest = split2(e)
            numer = numer + mm(kvt_ref[64:128, pl.ds(at, rows)], side(high, rest))
            return total + jnp.sum(e, axis=0, keepdims=True), numer

        total, numer = over_rows(wide_sums, (jnp.zeros((1, 128), F32), jnp.zeros((64, 256), F32)))
        mem_out = ((numer[:, 0:128] + numer[:, 128:256]) / total).astype(BF16)
        mem_dot = jnp.sum(mqo_t[64:128].astype(F32) * mem_out.astype(F32), axis=0, keepdims=True)
        share = 1.0 / total

        def wide_grads(at, rows, dq):
            p = ww_ref[pl.ds(at, rows), 0:128] * share
            dw = (p * (ww_ref[pl.ds(at, rows), 128:256] - mem_dot)).astype(BF16)
            ww_ref[pl.ds(at, rows), 0:128] = mm(side(dw, p.astype(BF16)), wide_back)
            return dq + mm(kvt_ref[0:64, pl.ds(at, rows)], dw)

        mem_dq = over_rows(wide_grads, jnp.zeros((64, 128), F32)) * scale
        dq_high, dq_rest = split2(mem_dq)
        mem_rows = jnp.concatenate([dq_high, mem_out, dq_rest], axis=0)

        def band(i, c):
            many = range(BAND_GROUP)
            slot = [i * BAND_GROUP + u for u in many]
            at = [pl.multiple_of(s * tile, tile) for s in slot]
            win = [pl.ds(a, 2 * tile) for a in at]
            qd = [qd_ref[pl.ds(a, tile), :] for a in at]
            qd_t = [qdt_ref[:, pl.ds(a, tile)] for a in at]
            rhs = [spread(x) for x in qd_t]
            near = [mm(kv_ref[win[u], :], rhs[u]) for u in many]
            far = [mm(mkv, rhs[u]) for u in many]
            p_near, p_far, pb_near, pb_far = [], [], [], []
            for u in many:
                s_near = jnp.where(
                    usable(at[u], 2 * tile, length), near[u][:, 0:128] + tb_ref[...], NEG_BIG
                )
                s_far = far[u][:, 0:128]
                high = jnp.maximum(
                    jnp.max(s_near, axis=0, keepdims=True), jnp.max(s_far, axis=0, keepdims=True)
                )
                e_near, e_far = jnp.exp(s_near - high), jnp.exp(s_far - high)
                inv = 1.0 / (
                    jnp.sum(e_near, axis=0, keepdims=True) + jnp.sum(e_far, axis=0, keepdims=True)
                )
                p_near.append(e_near * inv)
                p_far.append(e_far * inv)
                pb_near.append(p_near[u].astype(BF16))
                pb_far.append(p_far[u].astype(BF16))
            out = [
                mm(kvt_ref[64:128, win[u]], pb_near[u]) + mm(mkv_t[64:128], pb_far[u]) for u in many
            ]
            back = [stack(x) for x in qd]
            ds_near, db_near, db_far = [], [], []
            for u in many:
                out[u] = out[u].astype(BF16).astype(F32)
                row_dot = jnp.sum(qd_t[u][64:128].astype(F32) * out[u], axis=0, keepdims=True)
                ds_near.append(p_near[u] * (near[u][:, 128:256] - row_dot))
                db_near.append(ds_near[u].astype(BF16))
                db_far.append((p_far[u] * (far[u][:, 128:256] - row_dot)).astype(BF16))
            gb_ref[...] += sum(ds_near)
            dq = [mm(kvt_ref[0:64, win[u]], db_near[u]) + mm(mkv_t[0:64], db_far[u]) for u in many]
            d_near = [mm(side(db_near[u], pb_near[u]), back[u]) for u in many]
            d_far = [mm(side(db_far[u], pb_far[u]), back[u]) for u in many]
            gm_ref[...] += sum(d_far)
            parts = [d_near[0][0:tile]]
            for u in many[1:]:
                parts.append(d_near[u - 1][tile:] + d_near[u][0:tile])
            parts.append(d_near[-1][tile:])
            ww_ref[pl.ds(at[0], tile * (BAND_GROUP + 1)), 0:128] += jnp.concatenate(parts, axis=0)
            for u in many:
                pick = (gr_col == lane + at[u]).astype(F32)
                mine = jnp.max(pick, axis=0, keepdims=True)
                placed = mm(mem_rows, pick.astype(BF16))
                live = lane[0:1] + at[u] < length
                o = jnp.where(live, jnp.where(mine > 0.5, placed[64:128], out[u]), 0.0)
                d = dq[u] * scale + (placed[0:64] + placed[128:192])
                y_ref[slot[u], 0:tile, 128:256] = jnp.concatenate([d, o], axis=0).astype(BF16).T
            return c

        lax.fori_loop(0, slots // BAND_GROUP, band, 0)

        wide_bias = jnp.concatenate([gb_ref[...], jnp.zeros((128, 128), F32)], axis=0).T
        bias_sum = jnp.sum(shear(wide_bias, blk - 1, -1), axis=0, keepdims=True)[:, 0:256]
        b0 = bias_sum.astype(BF16).astype(F32)
        b1 = (bias_sum - b0).astype(BF16).astype(F32)
        b2 = bias_sum - b0 - b1
        bias_rows = jnp.concatenate(
            [b0, b1, b2, jnp.zeros((BIAS_ROWS - 3, 256), F32)], axis=0
        ).astype(BF16)

        mem_back = jnp.concatenate(split2(gm_ref[...]), axis=0)

        def finish(first_half):
            def body(i, c):
                at = pl.multiple_of(i * chunk, chunk)
                grads = ww_ref[pl.ds(pl.multiple_of(at + blk, blk), chunk), 0:128]
                if first_half:
                    pick = (wide_row == wide_sub + at).astype(BF16)
                    grads = grads + mm(side(pick, pick), mem_back)
                y_ref[pl.ds(i * GROUP, GROUP), 0:tile, 0:128] = grads.astype(BF16).reshape(
                    GROUP, tile, 128
                )
                for u in range(GROUP):
                    y_ref[i * GROUP + u, tile:, :] = bias_rows
                return c

            return body

        lax.fori_loop(0, steps // 2, finish(True), 0)
        lax.fori_loop(steps // 2, steps, finish(False), 0)


def vmem(shape, dtype):
    return pltpu.VMEM(shape, dtype)


def grant(frames):
    return pltpu.CompilerParams(vmem_limit_bytes=min(16 * frames // 2048, 60) * 1024 * 1024)


def core_call(by_head, rows, position_bias):
    slots, tile, _ = by_head.shape
    frames = slots * tile
    return pl.pallas_call(
        core_kernel,
        out_shape=jax.ShapeDtypeStruct((slots, tile + BIAS_ROWS, 256), BF16),
        scratch_shapes=[
            vmem((frames + tile, 128), BF16),
            vmem((128, frames + tile), BF16),
            vmem((frames, 128), BF16),
            vmem((128, frames), BF16),
            vmem((frames + tile, 256), F32),
            vmem((2 * tile, 128), F32),
            vmem((2 * tile, 128), F32),
            vmem((128, 128), F32),
        ],
        compiler_params=grant(frames),
    )(rows, position_bias, by_head)


def local(
    frame_queries, frame_keys, frame_values, cotangent, frame_mask, global_rows, position_bias
):
    slots = lax.axis_size("seq")
    tile, width = frame_queries.shape
    heads, span = position_bias.shape
    memory = global_rows.shape[0]
    frames = slots * tile

    hbm = pl.BlockSpec(memory_space=pltpu.MemorySpace.HBM)
    whole = pltpu.VMEM((tile, width), BF16)
    packed = pl.pallas_call(
        pack_kernel,
        out_shape=jax.ShapeDtypeStruct((slots, tile, 256), BF16),
        in_specs=[hbm] * 5,
        scratch_shapes=[
            pltpu.VMEM((1, tile), jnp.int32),
            whole,
            whole,
            whole,
            whole,
            pltpu.SemaphoreType.DMA((5,)),
        ],
        compiler_params=grant(frames),
    )(
        *(
            pltpu.with_memory_space_constraint(x, pltpu.MemorySpace.HBM)
            for x in (
                frame_mask.reshape(1, tile),
                frame_keys,
                frame_values,
                frame_queries,
                cotangent,
            )
        )
    )
    by_head = lax.all_to_all(packed, "seq", 0, 0, tiled=True)
    grads = core_call(by_head, global_rows.reshape(1, memory), position_bias)
    by_frame = lax.all_to_all(grads, "seq", 0, 0, tiled=True)
    rows = jax.ShapeDtypeStruct((tile, width), BF16)
    attended, dq, dk, dv, grad_bias = pl.pallas_call(
        unpack_kernel,
        out_shape=(rows, rows, rows, rows, jax.ShapeDtypeStruct((heads, span), F32)),
        compiler_params=grant(frames),
    )(by_frame)
    return (attended, dq, dk, dv, grad_bias)


def solution(mesh):
    return jax.shard_map(
        local,
        mesh=mesh,
        in_specs=(
            P(("groups", "seq"), None),
            P(("groups", "seq"), None),
            P(("groups", "seq"), None),
            P(("groups", "seq"), None),
            P(("groups", "seq")),
            P("groups"),
            P(),
        ),
        out_specs=(
            P(("groups", "seq"), None),
            P(("groups", "seq"), None),
            P(("groups", "seq"), None),
            P(("groups", "seq"), None),
            P("groups", None),
        ),
        check_vma=False,
    )
```

time: 106 us -> 76.1 us (0.72)
  Pallas kernels: 39.4 us -> 10.3 us
    pallas_call x1, Pallas kernels: 34.4 us -> 7.61 us  [core_call(): pl.pallas_call(core_kernel, out_shape=jax.ShapeDtypeStruct((slots, tile +...]
    pallas_call x1, Pallas kernels: 2.37 us -> 1.12 us  [local(): pl.pallas_call(unpack_kernel, out_shape=(rows, rows, rows, rows, jax.Shap...]
where the time goes in v2:
time: 76.1 us; the launch traced here: 75.8 us
  blocking collectives  64.9 us (85%)
  Pallas kernels  10.3 us (14%)
    all_to_all x1, blocking collectives, local(): by_frame = lax.all_to_all(grads, 'seq', 0, 0, tiled=True)  32.8 us
    all_to_all x1, blocking collectives, local(): by_head = lax.all_to_all(packed, 'seq', 0, 0, tiled=True)  32 us
    pallas_call x1, Pallas kernels, core_call(): pl.pallas_call(core_kernel, out_shape=jax.ShapeDtypeStruct((slots, tile +...  7.61 us
    pallas_call x1, Pallas kernels, local(): pl.pallas_call(pack_kernel, out_shape=jax.ShapeDtypeStruct((slots, tile,...  1.56 us

profile of v2, /device:TPU:0, one launch (start us, length us, event | category | flops | bytes accessed | tf_op | source)
XLA Modules:
  0.0 75.8 jit_solution(14244285738662238919)
XLA Ops:
  0.6 1.6 %shard_map.110 = bf16[16,128,256]{2,1,0:T(8,128)(2,1)S(1)} custom-call(s32[1,128]{1,0:T(1,128)} %bitcast.3, bf16[128,768]{1,0:T(8,128)(2,1)} %refs_1_.1, bf16[128,768]{1,0:T(8,128)(2,1)} %refs_2_.1, bf16[128,768]{1,0:T(8,128)(2,1)} %refs_3_.1, bf16[128,768]{1,0:T(8,128)(2,1)} %refs_4_.1), custom_call_target="tpu_custom_call" | custom-call | tf_op jit(solution)/shard_map/pallas_call | solution.py:358
  2.2 0.0 copy-start
  2.2 0.0 copy-start.1
  2.2 32.0 %all_to_all.10.x_ref = bf16[16,128,256]{2,1,0:T(8,128)(2,1)S(1)} all-to-all(bf16[16,128,256]{2,1,0:T(8,128)(2,1)S(1)} %shard_map.110), channel_id=1, replica_groups=mesh['groups'=2,'seq'=16] {'seq'}, dimensions={0} | all-to-all | bytes 2097152 | tf_op jit(solution)/shard_map/all_to_all | solution.py:383
  34.3 0.0 copy-done
  34.3 0.0 copy-done.1
  34.3 7.6 %shard_map.111 = bf16[16,136,256]{2,1,0:T(8,128)(2,1)S(1)} custom-call(s32[1,128]{1,0:T(1,128)S(1)} %bitcast.2, f32[12,255]{1,0:T(8,128)S(1)} %copy-done, bf16[16,128,256]{2,1,0:T(8,128)(2,1)S(1)} %all_to_all.10.x_ref), custom_call_target="tpu_custom_call" | custom-call | tf_op jit(solution)/shard_map/pallas_call | solution.py:330
  41.9 32.8 %all_to_all.11.in_ref = bf16[16,136,256]{2,1,0:T(8,128)(2,1)S(1)} all-to-all(bf16[16,136,256]{2,1,0:T(8,128)(2,1)S(1)} %shard_map.111), channel_id=1, replica_groups=mesh['groups'=2,'seq'=16] {'seq'}, dimensions={0} | all-to-all | bytes 2228224 | tf_op jit(solution)/shard_map/all_to_all | solution.py:385
  74.7 1.1 %shard_map.112 = (bf16[128,768]{1,0:T(8,128)(2,1)}, bf16[128,768]{1,0:T(8,128)(2,1)}, bf16[128,768]{1,0:T(8,128)(2,1)}, bf16[128,768]{1,0:T(8,128)(2,1)}, f32[12,255]{1,0:T(8,128)}) custom-call(bf16[16,136,256]{2,1,0:T(8,128)(2,1)S(1)} %all_to_all.11.in_ref), custom_call_target="tpu_custom_call" | custom-call | tf_op jit(solution)/shard_map/pallas_call | solution.py:387
Async XLA Ops:
  2.2 32.1 %copy-start = (f32[12,255]{1,0:T(8,128)S(1)}, f32[12,255]{1,0:T(8,128)}, u32[]{:S(2)}) copy-start(f32[12,255]{1,0:T(8,128)} %bias_ref.1) | copy-start | bytes 36724
  2.2 32.1 %copy-start.1 = (s32[128]{0:T(128)S(1)}, s32[128]{0:T(128)}, u32[]{:S(2)}) copy-start(s32[128]{0:T(128)} %param.12) | copy-start | bytes 1540

commit v3 on v2

--- a/solution.py
+++ b/solution.py
@@ -1,3 +1,5 @@
+import functools
+
 import jax
 import jax.numpy as jnp
 from jax import lax
@@ -10,6 +12,7 @@
 BIAS_ROWS = 8
 GROUP = 8
 BAND_GROUP = 16
+SKEW = 2
 BF16 = jnp.bfloat16
 F32 = jnp.float32
 
@@ -84,6 +87,18 @@
         gb_ref[h : h + 1, :] = whole[:, : gb_ref.shape[1]]
 
 
+def repeat(first, last, body, carry):
+    if last - first > 2:
+        return lax.fori_loop(first, last, body, carry)
+    for i in range(first, last):
+        carry = body(i, carry)
+    return carry
+
+
+def aligned(x, size):
+    return x if isinstance(x, int) else pl.multiple_of(x, size)
+
+
 def shear(x, first, step):
     rows, lanes = x.shape
     row = iota(x.shape, 0)
@@ -96,7 +111,7 @@
 
 
 def core_kernel(
-    rows_ref, bias_ref, x_ref, y_ref, kv_ref, kvt_ref, qd_ref, qdt_ref, ww_ref, tb_ref, gb_ref, gm_ref
+    rows_ref, bias_ref, x_ref, y_ref, kv_ref, kvt_ref, qd_ref, qdt_ref, ww_ref, tb_ref, gb_ref, gm_ref, pick_ref
 ):
     slots, tile, _ = x_ref.shape
     frames = slots * tile
@@ -106,6 +121,7 @@
     scale = 64 ** (-0.5)
     owner = lax.axis_index("seq")
     chunk = GROUP * tile
+    steps = slots // GROUP
 
     @pl.when(owner < heads)
     def _():
@@ -129,14 +145,17 @@
             )
 
         def over_rows(body, carry):
-            carry = lax.fori_loop(
-                0, slots // GROUP, lambda i, c: body(pl.multiple_of(i * chunk, chunk), chunk, c), carry
-            )
-            return body(frames, tile, carry)
+            carry = repeat(
+                0, steps - 1, lambda i, c: body(aligned(i * chunk, chunk), chunk, c), carry
+            )
+            return body(frames - chunk, chunk + tile, carry)
 
         def usable(at, rows, length):
             place = iota((rows, 128), 0) + (at - blk)
-            return (place >= 0) & (place < length)
+            inside = place < length
+            if isinstance(at, int) and at >= blk:
+                return inside
+            return (place >= 0) & inside
 
         zeros = jnp.zeros((blk, 128), BF16)
         kv_ref[0:blk, :] = zeros
@@ -151,15 +170,17 @@
         def prepare(first_half):
             def body(i, c):
                 count, mem = c
-                at = pl.multiple_of(i * chunk, chunk)
+                at = aligned(i * chunk, chunk)
                 x = x_ref[pl.ds(i * GROUP, GROUP)].reshape(chunk, 256)
-                kv_ref[pl.ds(pl.multiple_of(at + blk, blk), chunk), :] = x[:, 0:128]
+                kv_ref[pl.ds(aligned(at + blk, blk), chunk), :] = x[:, 0:128]
                 qd = x[:, 128:256].astype(F32)
                 alive = qd < 0.5 * DEAD
                 count = count + jnp.sum(alive.astype(F32), axis=0, keepdims=True)
                 keep = alive
                 if first_half:
-                    mem = mem + mm((wide_col == wide_lane + at).astype(BF16), x)
+                    pick = (wide_col == wide_lane + at).astype(BF16)
+                    pick_ref[:, pl.ds(at, chunk)] = pick
+                    mem = mem + mm(pick, x)
                     mine = mm((wide_row == wide_sub + at).astype(BF16), ones)
                     keep = alive & (mine < 0.5)
                 qd = jnp.where(wide_low, qd * scale, jnp.where(keep, qd, 0.0)).astype(BF16)
@@ -169,10 +190,9 @@
 
             return body
 
-        steps = slots // GROUP
         carry = (jnp.zeros((1, 128), F32), jnp.zeros((128, 256), F32))
-        carry = lax.fori_loop(0, steps // 2, prepare(True), carry)
-        count, mem = lax.fori_loop(steps // 2, steps, prepare(False), carry)
+        carry = repeat(0, steps // 2, prepare(True), carry)
+        count, mem = repeat(steps // 2, steps, prepare(False), carry)
         length = jnp.max(count[:, 64:65], axis=1, keepdims=True).astype(jnp.int32)
         mkv = mem[:, 0:128].astype(BF16)
         mqo = jnp.where(low_lane, mem[:, 128:256] * scale, mem[:, 128:256]).astype(BF16)
@@ -204,7 +224,6 @@
         def wide_sums(at, rows, c):
             total, numer = c
             e = jnp.exp(ww_ref[pl.ds(at, rows), 0:128] - top)
-            e = jnp.where(usable(at, rows, length), e, 0.0)
             ww_ref[pl.ds(at, rows), 0:128] = e
             high, rest = split2(e)
             numer = numer + mm(kvt_ref[64:128, pl.ds(at, rows)], side(high, rest))
@@ -223,67 +242,91 @@
 
         mem_dq = over_rows(wide_grads, jnp.zeros((64, 128), F32)) * scale
         dq_high, dq_rest = split2(mem_dq)
-        mem_rows = jnp.concatenate([dq_high, mem_out, dq_rest], axis=0)
-
-        def band(i, c):
-            many = range(BAND_GROUP)
-            slot = [i * BAND_GROUP + u for u in many]
-            at = [pl.multiple_of(s * tile, tile) for s in slot]
-            win = [pl.ds(a, 2 * tile) for a in at]
-            qd = [qd_ref[pl.ds(a, tile), :] for a in at]
-            qd_t = [qdt_ref[:, pl.ds(a, tile)] for a in at]
-            rhs = [spread(x) for x in qd_t]
-            near = [mm(kv_ref[win[u], :], rhs[u]) for u in many]
-            far = [mm(mkv, rhs[u]) for u in many]
-            p_near, p_far, pb_near, pb_far = [], [], [], []
-            for u in many:
-                s_near = jnp.where(
-                    usable(at[u], 2 * tile, length), near[u][:, 0:128] + tb_ref[...], NEG_BIG
-                )
-                s_far = far[u][:, 0:128]
-                high = jnp.maximum(
-                    jnp.max(s_near, axis=0, keepdims=True), jnp.max(s_far, axis=0, keepdims=True)
-                )
-                e_near, e_far = jnp.exp(s_near - high), jnp.exp(s_far - high)
-                inv = 1.0 / (
-                    jnp.sum(e_near, axis=0, keepdims=True) + jnp.sum(e_far, axis=0, keepdims=True)
-                )
-                p_near.append(e_near * inv)
-                p_far.append(e_far * inv)
-                pb_near.append(p_near[u].astype(BF16))
-                pb_far.append(p_far[u].astype(BF16))
-            out = [
-                mm(kvt_ref[64:128, win[u]], pb_near[u]) + mm(mkv_t[64:128], pb_far[u]) for u in many
-            ]
-            back = [stack(x) for x in qd]
-            ds_near, db_near, db_far = [], [], []
-            for u in many:
-                out[u] = out[u].astype(BF16).astype(F32)
-                row_dot = jnp.sum(qd_t[u][64:128].astype(F32) * out[u], axis=0, keepdims=True)
-                ds_near.append(p_near[u] * (near[u][:, 128:256] - row_dot))
-                db_near.append(ds_near[u].astype(BF16))
-                db_far.append((p_far[u] * (far[u][:, 128:256] - row_dot)).astype(BF16))
-            gb_ref[...] += sum(ds_near)
-            dq = [mm(kvt_ref[0:64, win[u]], db_near[u]) + mm(mkv_t[0:64], db_far[u]) for u in many]
-            d_near = [mm(side(db_near[u], pb_near[u]), back[u]) for u in many]
-            d_far = [mm(side(db_far[u], pb_far[u]), back[u]) for u in many]
-            gm_ref[...] += sum(d_far)
-            parts = [d_near[0][0:tile]]
-            for u in many[1:]:
-                parts.append(d_near[u - 1][tile:] + d_near[u][0:tile])
-            parts.append(d_near[-1][tile:])
-            ww_ref[pl.ds(at[0], tile * (BAND_GROUP + 1)), 0:128] += jnp.concatenate(parts, axis=0)
-            for u in many:
-                pick = (gr_col == lane + at[u]).astype(F32)
-                mine = jnp.max(pick, axis=0, keepdims=True)
-                placed = mm(mem_rows, pick.astype(BF16))
-                live = lane[0:1] + at[u] < length
-                o = jnp.where(live, jnp.where(mine > 0.5, placed[64:128], out[u]), 0.0)
-                d = dq[u] * scale + (placed[0:64] + placed[128:192])
-                y_ref[slot[u], 0:tile, 128:256] = jnp.concatenate([d, o], axis=0).astype(BF16).T
+        mem_rows = jnp.concatenate([dq_high, mem_out, dq_rest, jnp.ones((16, 128), BF16)], axis=0)
+
+        def scores(t):
+            t["qd_t"] = qdt_ref[:, pl.ds(t["at"], tile)]
+            rhs = spread(t["qd_t"])
+            t["near"], t["far"] = mm(kv_ref[t["win"], :], rhs), mm(mkv, rhs)
+
+        def softmax(t):
+            s_near = jnp.where(
+                usable(t["at"], 2 * tile, length), t["near"][:, 0:128] + tb_ref[...], NEG_BIG
+            )
+            s_far = t["far"][:, 0:128]
+            high = jnp.maximum(
+                jnp.max(s_near, axis=0, keepdims=True), jnp.max(s_far, axis=0, keepdims=True)
+            )
+            e_near, e_far = jnp.exp(s_near - high), jnp.exp(s_far - high)
+            inv = 1.0 / (
+                jnp.sum(e_near, axis=0, keepdims=True) + jnp.sum(e_far, axis=0, keepdims=True)
+            )
+            t["p_near"], t["p_far"] = e_near * inv, e_far * inv
+            t["pb_near"], t["pb_far"] = t["p_near"].astype(BF16), t["p_far"].astype(BF16)
+
+        def forward(t):
+            out = mm(kvt_ref[64:128, t["win"]], t["pb_near"]) + mm(mkv_t[64:128], t["pb_far"])
+            t["out"] = out.astype(BF16).astype(F32)
+
+        def score_grads(t):
+            row_dot = jnp.sum(t["qd_t"][64:128].astype(F32) * t["out"], axis=0, keepdims=True)
+            ds_near = t["p_near"] * (t["near"][:, 128:256] - row_dot)
+            ds_far = t["p_far"] * (t["far"][:, 128:256] - row_dot)
+            t["bias"] += ds_near
+            t["db_near"], t["db_far"] = ds_near.astype(BF16), ds_far.astype(BF16)
+
+        def backward(t):
+            back = stack(qd_ref[pl.ds(t["at"], tile), :])
+            dq = mm(kvt_ref[0:64, t["win"]], t["db_near"]) + mm(mkv_t[0:64], t["db_far"])
+            t["dq"] = dq * scale
+            t["d_near"] = mm(side(t["db_near"], t["pb_near"]), back)
+            t["d_far"] = mm(side(t["db_far"], t["pb_far"]), back)
+
+        def write(t):
+            d, o = t["dq"], t["out"]
+            if t["first_half"]:
+                placed = mm(mem_rows, pick_ref[:, pl.ds(t["at"], tile)])
+                o = jnp.where(placed[192:193] > 0.5, placed[64:128], o)
+                d = d + (placed[0:64] + placed[128:192])
+            o = jnp.where(lane[0:1] + t["at"] < length, o, 0.0)
+            y_ref[t["slot"], 0:tile, 128:256] = jnp.concatenate([d, o], axis=0).astype(BF16).T
+
+        stages = (scores, softmax, forward, score_grads, backward, write)
+
+        def band(first_half, i, c):
+            tiles = []
+            bias, tail, far = gb_ref[...], 0.0, gm_ref[...]
+            for u in range(BAND_GROUP):
+                slot = i * BAND_GROUP + u
+                at = aligned(slot * tile, tile)
+                half = slot < slots // 2 if first_half is None else first_half
+                tiles.append({"slot": slot, "at": at, "win": pl.ds(at, 2 * tile), "first_half": half})
+            for step in range(BAND_GROUP + SKEW * (len(stages) - 1)):
+                for k, stage in enumerate(stages):
+                    u = step - SKEW * k
+                    if not 0 <= u < BAND_GROUP:
+                        continue
+                    t = tiles[u]
+                    if stage is score_grads:
+                        t["bias"] = bias
+                    stage(t)
+                    if stage is score_grads:
+                        bias = t["bias"]
+                    if stage is backward:
+                        ww_ref[pl.ds(t["at"], tile), 0:128] += tail + t["d_near"][0:tile]
+                        tail = t["d_near"][tile:]
+                        far = far + t["d_far"]
+            ww_ref[pl.ds(aligned(tiles[-1]["at"] + tile, tile), tile), 0:128] += tail
+            gb_ref[...] = bias
+            gm_ref[...] = far
             return c
 
-        lax.fori_loop(0, slots // BAND_GROUP, band, 0)
+        rounds = slots // BAND_GROUP
+        if rounds == 1:
+            band(None, 0, 0)
+        else:
+            repeat(0, rounds // 2, functools.partial(band, True), 0)
+            repeat(rounds // 2, rounds, functools.partial(band, False), 0)
 
         wide_bias = jnp.concatenate([gb_ref[...], jnp.zeros((128, 128), F32)], axis=0).T
         bias_sum = jnp.sum(shear(wide_bias, blk - 1, -1), axis=0, keepdims=True)[:, 0:256]
@@ -298,8 +341,8 @@
 
         def finish(first_half):
             def body(i, c):
-                at = pl.multiple_of(i * chunk, chunk)
-                grads = ww_ref[pl.ds(pl.multiple_of(at + blk, blk), chunk), 0:128]
+                at = aligned(i * chunk, chunk)
+                grads = ww_ref[pl.ds(aligned(at + blk, blk), chunk), 0:128]
                 if first_half:
                     pick = (wide_row == wide_sub + at).astype(BF16)
                     grads = grads + mm(side(pick, pick), mem_back)
@@ -312,8 +355,8 @@
 
             return body
 
-        lax.fori_loop(0, steps // 2, finish(True), 0)
-        lax.fori_loop(steps // 2, steps, finish(False), 0)
+        repeat(0, steps // 2, finish(True), 0)
+        repeat(steps // 2, steps, finish(False), 0)
 
 
 def vmem(shape, dtype):
@@ -339,6 +382,7 @@
             vmem((2 * tile, 128), F32),
             vmem((2 * tile, 128), F32),
             vmem((128, 128), F32),
+            vmem((128, frames // 2), BF16),
         ],
         compiler_params=grant(frames),
     )(rows, position_bias, by_head)

time: 76.1 us -> 74.5 us (0.979)
  Pallas kernels: 10.3 us -> 8.7 us
    pallas_call x1, Pallas kernels: 7.61 us -> 6.02 us  [core_call(): pl.pallas_call(core_kernel, out_shape=jax.ShapeDtypeStruct((slots, tile +...]
where the time goes in v3:
time: 74.5 us; the launch traced here: 74.2 us
  blocking collectives  64.9 us (87%)
  Pallas kernels  8.7 us (12%)
    all_to_all x1, blocking collectives, local(): by_frame = lax.all_to_all(grads, 'seq', 0, 0, tiled=True)  32.8 us
    all_to_all x1, blocking collectives, local(): by_head = lax.all_to_all(packed, 'seq', 0, 0, tiled=True)  32 us
    pallas_call x1, Pallas kernels, core_call(): pl.pallas_call(core_kernel, out_shape=jax.ShapeDtypeStruct((slots, tile +...  6.02 us
    pallas_call x1, Pallas kernels, local(): pl.pallas_call(pack_kernel, out_shape=jax.ShapeDtypeStruct((slots, tile,...  1.56 us

profile of v3, /device:TPU:0, one launch (start us, length us, event | category | flops | bytes accessed | tf_op | source)
XLA Modules:
  0.0 74.2 jit_solution(6041018227726647214)
XLA Ops:
  0.6 1.6 %shard_map.110 = bf16[16,128,256]{2,1,0:T(8,128)(2,1)S(1)} custom-call(s32[1,128]{1,0:T(1,128)} %bitcast.3, bf16[128,768]{1,0:T(8,128)(2,1)} %refs_1_.1, bf16[128,768]{1,0:T(8,128)(2,1)} %refs_2_.1, bf16[128,768]{1,0:T(8,128)(2,1)} %refs_3_.1, bf16[128,768]{1,0:T(8,128)(2,1)} %refs_4_.1), custom_call_target="tpu_custom_call" | custom-call | tf_op jit(solution)/shard_map/pallas_call | solution.py:402
  2.2 0.0 copy-start
  2.2 0.0 copy-start.1
  2.2 32.0 %all_to_all.10.x_ref = bf16[16,128,256]{2,1,0:T(8,128)(2,1)S(1)} all-to-all(bf16[16,128,256]{2,1,0:T(8,128)(2,1)S(1)} %shard_map.110), channel_id=1, replica_groups=mesh['groups'=2,'seq'=16] {'seq'}, dimensions={0} | all-to-all | bytes 2097152 | tf_op jit(solution)/shard_map/all_to_all | solution.py:427
  34.3 0.0 copy-done
  34.3 0.0 copy-done.1
  34.3 6.0 %shard_map.111 = bf16[16,136,256]{2,1,0:T(8,128)(2,1)S(1)} custom-call(s32[1,128]{1,0:T(1,128)S(1)} %bitcast.2, f32[12,255]{1,0:T(8,128)S(1)} %copy-done, bf16[16,128,256]{2,1,0:T(8,128)(2,1)S(1)} %all_to_all.10.x_ref), custom_call_target="tpu_custom_call" | custom-call | tf_op jit(solution)/shard_map/pallas_call | solution.py:373
  40.3 32.8 %all_to_all.11.in_ref = bf16[16,136,256]{2,1,0:T(8,128)(2,1)S(1)} all-to-all(bf16[16,136,256]{2,1,0:T(8,128)(2,1)S(1)} %shard_map.111), channel_id=1, replica_groups=mesh['groups'=2,'seq'=16] {'seq'}, dimensions={0} | all-to-all | bytes 2228224 | tf_op jit(solution)/shard_map/all_to_all | solution.py:429
  73.1 1.1 %shard_map.112 = (bf16[128,768]{1,0:T(8,128)(2,1)}, bf16[128,768]{1,0:T(8,128)(2,1)}, bf16[128,768]{1,0:T(8,128)(2,1)}, bf16[128,768]{1,0:T(8,128)(2,1)}, f32[12,255]{1,0:T(8,128)}) custom-call(bf16[16,136,256]{2,1,0:T(8,128)(2,1)S(1)} %all_to_all.11.in_ref), custom_call_target="tpu_custom_call" | custom-call | tf_op jit(solution)/shard_map/pallas_call | solution.py:431
Async XLA Ops:
  2.2 32.1 %copy-start = (f32[12,255]{1,0:T(8,128)S(1)}, f32[12,255]{1,0:T(8,128)}, u32[]{:S(2)}) copy-start(f32[12,255]{1,0:T(8,128)} %bias_ref.1) | copy-start | bytes 36724
  2.2 32.1 %copy-start.1 = (s32[128]{0:T(128)S(1)}, s32[128]{0:T(128)}, u32[]{:S(2)}) copy-start(s32[128]{0:T(128)} %param.12) | copy-start | bytes 1540

commit v4 on v3

--- a/solution.py
+++ b/solution.py
@@ -12,7 +12,10 @@
 BIAS_ROWS = 8
 GROUP = 8
 BAND_GROUP = 16
-SKEW = 2
+SKEW = 4
+WIDE_FIRST = 0
+WIDE_TILES = 4
+WIDE_STEP = 5
 BF16 = jnp.bfloat16
 F32 = jnp.float32
 
@@ -111,7 +114,7 @@
 
 
 def core_kernel(
-    rows_ref, bias_ref, x_ref, y_ref, kv_ref, kvt_ref, qd_ref, qdt_ref, ww_ref, tb_ref, gb_ref, gm_ref, pick_ref
+    rows_ref, bias_ref, x_ref, y_ref, kv_ref, kvt_ref, qdt_ref, ww_ref, tb_ref, gb_ref, gm_ref, pick_ref, keep_ref
 ):
     slots, tile, _ = x_ref.shape
     frames = slots * tile
@@ -160,12 +163,12 @@
         zeros = jnp.zeros((blk, 128), BF16)
         kv_ref[0:blk, :] = zeros
         kv_ref[frames + blk :, :] = zeros
-        wide_low = iota((chunk, 128), 1) < 64
         wide_sub = iota((chunk, 128), 0)
         wide_lane = iota((128, chunk), 1)
         wide_row = jnp.broadcast_to(gr_row[0:1], (chunk, memory))
         wide_col = jnp.concatenate([gr_col] * GROUP, axis=1)
-        ones = jnp.ones((memory, 128), BF16)
+        ones = jnp.ones((16, memory), BF16)
+        scales = jnp.where(iota((1, 128), 1) < 64, scale, 1.0).astype(BF16)
 
         def prepare(first_half):
             def body(i, c):
@@ -173,27 +176,24 @@
                 at = aligned(i * chunk, chunk)
                 x = x_ref[pl.ds(i * GROUP, GROUP)].reshape(chunk, 256)
                 kv_ref[pl.ds(aligned(at + blk, blk), chunk), :] = x[:, 0:128]
-                qd = x[:, 128:256].astype(F32)
-                alive = qd < 0.5 * DEAD
-                count = count + jnp.sum(alive.astype(F32), axis=0, keepdims=True)
-                keep = alive
+                qd_t = (x[:, 128:256] * scales).T
+                qdt_ref[:, pl.ds(at, chunk)] = qd_t
+                alive = (qd_t[64:80].astype(F32)[0:1] < 0.5 * DEAD).astype(F32)
                 if first_half:
                     pick = (wide_col == wide_lane + at).astype(BF16)
                     pick_ref[:, pl.ds(at, chunk)] = pick
                     mem = mem + mm(pick, x)
-                    mine = mm((wide_row == wide_sub + at).astype(BF16), ones)
-                    keep = alive & (mine < 0.5)
-                qd = jnp.where(wide_low, qd * scale, jnp.where(keep, qd, 0.0)).astype(BF16)
-                qd_ref[pl.ds(at, chunk), :] = qd
-                qdt_ref[:, pl.ds(at, chunk)] = qd.T
-                return count, mem
+                    keep_ref[:, pl.ds(at, chunk)] = alive - mm(ones, pick)[0:1]
+                else:
+                    keep_ref[:, pl.ds(at, chunk)] = alive
+                return count + jnp.sum(alive, axis=1, keepdims=True), mem
 
             return body
 
-        carry = (jnp.zeros((1, 128), F32), jnp.zeros((128, 256), F32))
+        carry = (jnp.zeros((1, 1), F32), jnp.zeros((128, 256), F32))
         carry = repeat(0, steps // 2, prepare(True), carry)
         count, mem = repeat(steps // 2, steps, prepare(False), carry)
-        length = jnp.max(count[:, 64:65], axis=1, keepdims=True).astype(jnp.int32)
+        length = count.astype(jnp.int32)
         mkv = mem[:, 0:128].astype(BF16)
         mqo = jnp.where(low_lane, mem[:, 128:256] * scale, mem[:, 128:256]).astype(BF16)
         mkv_t = mkv.T
@@ -219,30 +219,39 @@
             ww_ref[pl.ds(at, rows), 128:256] = both[:, 128:256]
             return jnp.maximum(top, jnp.max(w, axis=0, keepdims=True))
 
-        top = over_rows(wide_scores, jnp.full((1, 128), NEG_BIG, F32))
-
         def wide_sums(at, rows, c):
             total, numer = c
-            e = jnp.exp(ww_ref[pl.ds(at, rows), 0:128] - top)
+            e = jnp.exp(ww_ref[pl.ds(at, rows), 0:128] - wide["top"])
             ww_ref[pl.ds(at, rows), 0:128] = e
             high, rest = split2(e)
             numer = numer + mm(kvt_ref[64:128, pl.ds(at, rows)], side(high, rest))
             return total + jnp.sum(e, axis=0, keepdims=True), numer
 
-        total, numer = over_rows(wide_sums, (jnp.zeros((1, 128), F32), jnp.zeros((64, 256), F32)))
-        mem_out = ((numer[:, 0:128] + numer[:, 128:256]) / total).astype(BF16)
-        mem_dot = jnp.sum(mqo_t[64:128].astype(F32) * mem_out.astype(F32), axis=0, keepdims=True)
-        share = 1.0 / total
+        def wide_out():
+            total, numer = wide["sums"]
+            mem_out = ((numer[:, 0:128] + numer[:, 128:256]) / total).astype(BF16)
+            wide["out"] = mem_out
+            wide["dot"] = jnp.sum(
+                mqo_t[64:128].astype(F32) * mem_out.astype(F32), axis=0, keepdims=True
+            )
+            wide["share"] = 1.0 / total
 
         def wide_grads(at, rows, dq):
-            p = ww_ref[pl.ds(at, rows), 0:128] * share
-            dw = (p * (ww_ref[pl.ds(at, rows), 128:256] - mem_dot)).astype(BF16)
+            p = ww_ref[pl.ds(at, rows), 0:128] * wide["share"]
+            dw = (p * (ww_ref[pl.ds(at, rows), 128:256] - wide["dot"])).astype(BF16)
             ww_ref[pl.ds(at, rows), 0:128] = mm(side(dw, p.astype(BF16)), wide_back)
             return dq + mm(kvt_ref[0:64, pl.ds(at, rows)], dw)
 
-        mem_dq = over_rows(wide_grads, jnp.zeros((64, 128), F32)) * scale
-        dq_high, dq_rest = split2(mem_dq)
-        mem_rows = jnp.concatenate([dq_high, mem_out, dq_rest, jnp.ones((16, 128), BF16)], axis=0)
+        def wide_rows():
+            high, rest = split2(wide["dq"] * scale)
+            wide["rows"] = jnp.concatenate([high, wide["out"], rest], axis=0)
+
+        wide = {
+            "top": jnp.full((1, 128), NEG_BIG, F32),
+            "sums": (jnp.zeros((1, 128), F32), jnp.zeros((64, 256), F32)),
+            "dq": jnp.zeros((64, 128), F32),
+        }
+        passes = (("top", wide_scores, None), ("sums", wide_sums, wide_out), ("dq", wide_grads, wide_rows))
 
         def scores(t):
             t["qd_t"] = qdt_ref[:, pl.ds(t["at"], tile)]
@@ -258,7 +267,7 @@
                 jnp.max(s_near, axis=0, keepdims=True), jnp.max(s_far, axis=0, keepdims=True)
             )
             e_near, e_far = jnp.exp(s_near - high), jnp.exp(s_far - high)
-            inv = 1.0 / (
+            inv = keep_ref[:, pl.ds(t["at"], tile)] / (
                 jnp.sum(e_near, axis=0, keepdims=True) + jnp.sum(e_far, axis=0, keepdims=True)
             )
             t["p_near"], t["p_far"] = e_near * inv, e_far * inv
@@ -276,7 +285,7 @@
             t["db_near"], t["db_far"] = ds_near.astype(BF16), ds_far.astype(BF16)
 
         def backward(t):
-            back = stack(qd_ref[pl.ds(t["at"], tile), :])
+            back = stack(x_ref[t["slot"], :, 128:256] * scales)
             dq = mm(kvt_ref[0:64, t["win"]], t["db_near"]) + mm(mkv_t[0:64], t["db_far"])
             t["dq"] = dq * scale
             t["d_near"] = mm(side(t["db_near"], t["pb_near"]), back)
@@ -285,15 +294,14 @@
         def write(t):
             d, o = t["dq"], t["out"]
             if t["first_half"]:
-                placed = mm(mem_rows, pick_ref[:, pl.ds(t["at"], tile)])
-                o = jnp.where(placed[192:193] > 0.5, placed[64:128], o)
+                placed = mm(wide["rows"], pick_ref[:, pl.ds(t["at"], tile)])
+                o = o + placed[64:128]
                 d = d + (placed[0:64] + placed[128:192])
-            o = jnp.where(lane[0:1] + t["at"] < length, o, 0.0)
             y_ref[t["slot"], 0:tile, 128:256] = jnp.concatenate([d, o], axis=0).astype(BF16).T
 
         stages = (scores, softmax, forward, score_grads, backward, write)
 
-        def band(first_half, i, c):
+        def band(first_half, between, i, c):
             tiles = []
             bias, tail, far = gb_ref[...], 0.0, gm_ref[...]
             for u in range(BAND_GROUP):
@@ -302,6 +310,8 @@
                 half = slot < slots // 2 if first_half is None else first_half
                 tiles.append({"slot": slot, "at": at, "win": pl.ds(at, 2 * tile), "first_half": half})
             for step in range(BAND_GROUP + SKEW * (len(stages) - 1)):
+                for work in between.get(step, ()):
+                    work()
                 for k, stage in enumerate(stages):
                     u = step - SKEW * k
                     if not 0 <= u < BAND_GROUP:
@@ -323,10 +333,27 @@
 
         rounds = slots // BAND_GROUP
         if rounds == 1:
-            band(None, 0, 0)
+            between = {}
+            part = WIDE_TILES * tile
+            cuts = list(range(0, frames, part))
+            for k, (name, body, after) in enumerate(passes):
+                for j, at in enumerate(cuts):
+
+                    def work(name=name, body=body, at=at, last=j == len(cuts) - 1, after=after):
+                        wide[name] = body(at, part + tile if last else part, wide[name])
+                        if last and after is not None:
+                            after()
+
+                    step = WIDE_FIRST + k * WIDE_STEP + j * WIDE_STEP // len(cuts)
+                    between.setdefault(step, []).append(work)
+            band(None, between, 0, 0)
         else:
-            repeat(0, rounds // 2, functools.partial(band, True), 0)
-            repeat(rounds // 2, rounds, functools.partial(band, False), 0)
+            for name, body, after in passes:
+                wide[name] = over_rows(body, wide[name])
+                if after is not None:
+                    after()
+            repeat(0, rounds // 2, functools.partial(band, True, {}), 0)
+            repeat(rounds // 2, rounds, functools.partial(band, False, {}), 0)
 
         wide_bias = jnp.concatenate([gb_ref[...], jnp.zeros((128, 128), F32)], axis=0).T
         bias_sum = jnp.sum(shear(wide_bias, blk - 1, -1), axis=0, keepdims=True)[:, 0:256]
@@ -376,13 +403,13 @@
         scratch_shapes=[
             vmem((frames + tile, 128), BF16),
             vmem((128, frames + tile), BF16),
-            vmem((frames, 128), BF16),
             vmem((128, frames), BF16),
             vmem((frames + tile, 256), F32),
             vmem((2 * tile, 128), F32),
             vmem((2 * tile, 128), F32),
             vmem((128, 128), F32),
             vmem((128, frames // 2), BF16),
+            vmem((1, frames), F32),
         ],
         compiler_params=grant(frames),
     )(rows, position_bias, by_head)

time: 74.5 us -> 73.8 us (level)
  no operation moved by 1% of the time
where the time goes in v4:
time: 73.8 us; the launch traced here: 73.6 us
  blocking collectives  64.9 us (88%)
  Pallas kernels  8.06 us (11%)
    all_to_all x1, blocking collectives, local(): by_frame = lax.all_to_all(grads, 'seq', 0, 0, tiled=True)  32.8 us
    all_to_all x1, blocking collectives, local(): by_head = lax.all_to_all(packed, 'seq', 0, 0, tiled=True)  32 us
    pallas_call x1, Pallas kernels, core_call(): pl.pallas_call(core_kernel, out_shape=jax.ShapeDtypeStruct((slots, tile +...  5.38 us
    pallas_call x1, Pallas kernels, local(): pl.pallas_call(pack_kernel, out_shape=jax.ShapeDtypeStruct((slots, tile,...  1.56 us

profile of v4, /device:TPU:0, one launch (start us, length us, event | category | flops | bytes accessed | tf_op | source)
XLA Modules:
  0.0 73.6 jit_solution(8826571625043232078)
XLA Ops:
  0.6 1.6 %shard_map.110 = bf16[16,128,256]{2,1,0:T(8,128)(2,1)S(1)} custom-call(s32[1,128]{1,0:T(1,128)} %bitcast.3, bf16[128,768]{1,0:T(8,128)(2,1)} %refs_1_.1, bf16[128,768]{1,0:T(8,128)(2,1)} %refs_2_.1, bf16[128,768]{1,0:T(8,128)(2,1)} %refs_3_.1, bf16[128,768]{1,0:T(8,128)(2,1)} %refs_4_.1), custom_call_target="tpu_custom_call" | custom-call | tf_op jit(solution)/shard_map/pallas_call | solution.py:429
  2.2 0.0 copy-start
  2.2 0.0 copy-start.1
  2.2 32.0 %all_to_all.10.x_ref = bf16[16,128,256]{2,1,0:T(8,128)(2,1)S(1)} all-to-all(bf16[16,128,256]{2,1,0:T(8,128)(2,1)S(1)} %shard_map.110), channel_id=1, replica_groups=mesh['groups'=2,'seq'=16] {'seq'}, dimensions={0} | all-to-all | bytes 2097152 | tf_op jit(solution)/shard_map/all_to_all | solution.py:454
  34.3 0.0 copy-done
  34.3 0.0 copy-done.1
  34.3 5.4 %shard_map.111 = bf16[16,136,256]{2,1,0:T(8,128)(2,1)S(1)} custom-call(s32[1,128]{1,0:T(1,128)S(1)} %bitcast.2, f32[12,255]{1,0:T(8,128)S(1)} %copy-done, bf16[16,128,256]{2,1,0:T(8,128)(2,1)S(1)} %all_to_all.10.x_ref), custom_call_target="tpu_custom_call" | custom-call | tf_op jit(solution)/shard_map/pallas_call | solution.py:400
  39.6 32.8 %all_to_all.11.in_ref = bf16[16,136,256]{2,1,0:T(8,128)(2,1)S(1)} all-to-all(bf16[16,136,256]{2,1,0:T(8,128)(2,1)S(1)} %shard_map.111), channel_id=1, replica_groups=mesh['groups'=2,'seq'=16] {'seq'}, dimensions={0} | all-to-all | bytes 2228224 | tf_op jit(solution)/shard_map/all_to_all | solution.py:456
  72.5 1.1 %shard_map.112 = (bf16[128,768]{1,0:T(8,128)(2,1)}, bf16[128,768]{1,0:T(8,128)(2,1)}, bf16[128,768]{1,0:T(8,128)(2,1)}, bf16[128,768]{1,0:T(8,128)(2,1)}, f32[12,255]{1,0:T(8,128)}) custom-call(bf16[16,136,256]{2,1,0:T(8,128)(2,1)S(1)} %all_to_all.11.in_ref), custom_call_target="tpu_custom_call" | custom-call | tf_op jit(solution)/shard_map/pallas_call | solution.py:458
Async XLA Ops:
  2.2 32.1 %copy-start = (f32[12,255]{1,0:T(8,128)S(1)}, f32[12,255]{1,0:T(8,128)}, u32[]{:S(2)}) copy-start(f32[12,255]{1,0:T(8,128)} %bias_ref.1) | copy-start | bytes 36724
  2.2 32.1 %copy-start.1 = (s32[128]{0:T(128)S(1)}, s32[128]{0:T(128)}, u32[]{:S(2)}) copy-start(s32[128]{0:T(128)} %param.12) | copy-start | bytes 1540

commit v5 on v4

--- a/solution.py
+++ b/solution.py
@@ -14,7 +14,7 @@
 BAND_GROUP = 16
 SKEW = 4
 WIDE_FIRST = 0
-WIDE_TILES = 4
+WIDE_TILES = 2
 WIDE_STEP = 5
 BF16 = jnp.bfloat16
 F32 = jnp.float32
@@ -59,17 +59,19 @@
         copy.wait()
     for i in range(pairs):
         at = slice(128 * i, 128 * (i + 1))
+        even, odd = 2 * i, 2 * i + 1
         k, v = k_ref[:, at], v_ref[:, at]
-        out_ref[2 * i, :, 0:128] = jnp.where(low, k, swap_halves(v))
-        out_ref[2 * i + 1, :, 0:128] = jnp.where(low, swap_halves(k), v)
+        out_ref[even, :, 0:128] = jnp.where(low, k, swap_halves(v))
+        out_ref[odd, :, 0:128] = jnp.where(low, swap_halves(k), v)
     for copy in copies[3:]:
         copy.wait()
     alive = iota((rows, 128), 0) < jnp.sum(mask_ref[...])
     for i in range(pairs):
         at = slice(128 * i, 128 * (i + 1))
         q, g = q_ref[:, at], jnp.where(alive, g_ref[:, at], jnp.asarray(DEAD, BF16))
-        out_ref[2 * i, :, 128:256] = jnp.where(low, q, swap_halves(g))
-        out_ref[2 * i + 1, :, 128:256] = jnp.where(low, swap_halves(q), g)
+        even, odd = 2 * i, 2 * i + 1
+        out_ref[even, :, 128:256] = jnp.where(low, q, swap_halves(g))
+        out_ref[odd, :, 128:256] = jnp.where(low, swap_halves(q), g)
 
 
 def unpack_kernel(in_ref, att_ref, dq_ref, dk_ref, dv_ref, gb_ref):
@@ -78,15 +80,17 @@
     low = iota((rows, 128), 1) < 64
     for i in range(pairs):
         at = slice(128 * i, 128 * (i + 1))
-        a, b = in_ref[2 * i, :rows, 0:128], in_ref[2 * i + 1, :rows, 0:128]
+        even, odd = 2 * i, 2 * i + 1
+        a, b = in_ref[even, :rows, :], in_ref[odd, :rows, :]
         dk_ref[:, at] = jnp.where(low, a, swap_halves(b))
         dv_ref[:, at] = jnp.where(low, swap_halves(a), b)
-        a, b = in_ref[2 * i, :rows, 128:256], in_ref[2 * i + 1, :rows, 128:256]
+        a, b = in_ref[even, rows : 2 * rows, :], in_ref[odd, rows : 2 * rows, :]
         dq_ref[:, at] = jnp.where(low, a, swap_halves(b))
         att_ref[:, at] = jnp.where(low, swap_halves(a), b)
     for h in range(2 * pairs):
-        parts = in_ref[h, rows:, :].astype(F32)
-        whole = parts[0:1] + parts[1:2] + parts[2:3]
+        parts = in_ref[h, 2 * rows :, :].astype(F32)
+        whole = parts[0:2] + parts[2:4] + parts[4:6]
+        whole = jnp.concatenate([whole[0:1], whole[1:2]], axis=1)
         gb_ref[h : h + 1, :] = whole[:, : gb_ref.shape[1]]
 
 
@@ -297,7 +301,7 @@
                 placed = mm(wide["rows"], pick_ref[:, pl.ds(t["at"], tile)])
                 o = o + placed[64:128]
                 d = d + (placed[0:64] + placed[128:192])
-            y_ref[t["slot"], 0:tile, 128:256] = jnp.concatenate([d, o], axis=0).astype(BF16).T
+            y_ref[t["slot"], tile : 2 * tile, :] = jnp.concatenate([d, o], axis=0).astype(BF16).T
 
         stages = (scores, softmax, forward, score_grads, backward, write)
 
@@ -360,9 +364,9 @@
         b0 = bias_sum.astype(BF16).astype(F32)
         b1 = (bias_sum - b0).astype(BF16).astype(F32)
         b2 = bias_sum - b0 - b1
-        bias_rows = jnp.concatenate(
-            [b0, b1, b2, jnp.zeros((BIAS_ROWS - 3, 256), F32)], axis=0
-        ).astype(BF16)
+        bias_rows = [b[:, at : at + 128] for b in (b0, b1, b2) for at in (0, 128)]
+        bias_rows = jnp.concatenate(bias_rows + [jnp.zeros((BIAS_ROWS - 6, 128), F32)], axis=0)
+        bias_rows = bias_rows.astype(BF16)
 
         mem_back = jnp.concatenate(split2(gm_ref[...]), axis=0)
 
@@ -373,11 +377,11 @@
                 if first_half:
                     pick = (wide_row == wide_sub + at).astype(BF16)
                     grads = grads + mm(side(pick, pick), mem_back)
-                y_ref[pl.ds(i * GROUP, GROUP), 0:tile, 0:128] = grads.astype(BF16).reshape(
+                y_ref[pl.ds(i * GROUP, GROUP), 0:tile, :] = grads.astype(BF16).reshape(
                     GROUP, tile, 128
                 )
                 for u in range(GROUP):
-                    y_ref[i * GROUP + u, tile:, :] = bias_rows
+                    y_ref[i * GROUP + u, 2 * tile :, :] = bias_rows
                 return c
 
             return body
@@ -399,7 +403,7 @@
     frames = slots * tile
     return pl.pallas_call(
         core_kernel,
-        out_shape=jax.ShapeDtypeStruct((slots, tile + BIAS_ROWS, 256), BF16),
+        out_shape=jax.ShapeDtypeStruct((slots, 2 * tile + BIAS_ROWS, 128), BF16),
         scratch_shapes=[
             vmem((frames + tile, 128), BF16),
             vmem((128, frames + tile), BF16),

time: 73.8 us -> 73.2 us (level)
  no operation moved by 1% of the time
where the time goes in v5:
time: 73.2 us; the launch traced here: 73 us
  blocking collectives  64.3 us (88%)
  Pallas kernels  7.99 us (11%)
    all_to_all x1, blocking collectives, local(): by_frame = lax.all_to_all(grads, 'seq', 0, 0, tiled=True)  32.3 us
    all_to_all x1, blocking collectives, local(): by_head = lax.all_to_all(packed, 'seq', 0, 0, tiled=True)  32 us
    pallas_call x1, Pallas kernels, core_call(): pl.pallas_call(core_kernel, out_shape=jax.ShapeDtypeStruct((slots, 2 * ti...  5.31 us
    pallas_call x1, Pallas kernels, local(): pl.pallas_call(pack_kernel, out_shape=jax.ShapeDtypeStruct((slots, tile,...  1.56 us

profile of v5, /device:TPU:0, one launch (start us, length us, event | category | flops | bytes accessed | tf_op | source)
XLA Modules:
  0.0 73.0 jit_solution(15369838183444562191)
XLA Ops:
  0.6 1.6 %shard_map.110 = bf16[16,128,256]{2,1,0:T(8,128)(2,1)S(1)} custom-call(s32[1,128]{1,0:T(1,128)} %bitcast.3, bf16[128,768]{1,0:T(8,128)(2,1)} %refs_1_.1, bf16[128,768]{1,0:T(8,128)(2,1)} %refs_2_.1, bf16[128,768]{1,0:T(8,128)(2,1)} %refs_3_.1, bf16[128,768]{1,0:T(8,128)(2,1)} %refs_4_.1), custom_call_target="tpu_custom_call" | custom-call | tf_op jit(solution)/shard_map/pallas_call | solution.py:433
  2.2 0.0 copy-start
  2.2 0.0 copy-start.1
  2.2 32.0 %all_to_all.10.x_ref = bf16[16,128,256]{2,1,0:T(8,128)(2,1)S(1)} all-to-all(bf16[16,128,256]{2,1,0:T(8,128)(2,1)S(1)} %shard_map.110), channel_id=1, replica_groups=mesh['groups'=2,'seq'=16] {'seq'}, dimensions={0} | all-to-all | bytes 2097152 | tf_op jit(solution)/shard_map/all_to_all | solution.py:458
  34.3 0.0 copy-done
  34.3 0.0 copy-done.1
  34.3 5.3 %shard_map.111 = bf16[16,264,128]{2,1,0:T(8,128)(2,1)S(1)} custom-call(s32[1,128]{1,0:T(1,128)S(1)} %bitcast.2, f32[12,255]{1,0:T(8,128)S(1)} %copy-done, bf16[16,128,256]{2,1,0:T(8,128)(2,1)S(1)} %all_to_all.10.x_ref), custom_call_target="tpu_custom_call" | custom-call | tf_op jit(solution)/shard_map/pallas_call | solution.py:404
  39.6 32.3 %all_to_all.11.in_ref = bf16[16,264,128]{2,1,0:T(8,128)(2,1)S(1)} all-to-all(bf16[16,264,128]{2,1,0:T(8,128)(2,1)S(1)} %shard_map.111), channel_id=1, replica_groups=mesh['groups'=2,'seq'=16] {'seq'}, dimensions={0} | all-to-all | bytes 2162688 | tf_op jit(solution)/shard_map/all_to_all | solution.py:460
  71.9 1.1 %shard_map.112 = (bf16[128,768]{1,0:T(8,128)(2,1)}, bf16[128,768]{1,0:T(8,128)(2,1)}, bf16[128,768]{1,0:T(8,128)(2,1)}, bf16[128,768]{1,0:T(8,128)(2,1)}, f32[12,255]{1,0:T(8,128)}) custom-call(bf16[16,264,128]{2,1,0:T(8,128)(2,1)S(1)} %all_to_all.11.in_ref), custom_call_target="tpu_custom_call" | custom-call | tf_op jit(solution)/shard_map/pallas_call | solution.py:462
Async XLA Ops:
  2.2 32.1 %copy-start = (f32[12,255]{1,0:T(8,128)S(1)}, f32[12,255]{1,0:T(8,128)}, u32[]{:S(2)}) copy-start(f32[12,255]{1,0:T(8,128)} %bias_ref.1) | copy-start | bytes 36724
  2.2 32.1 %copy-start.1 = (s32[128]{0:T(128)S(1)}, s32[128]{0:T(128)}, u32[]{:S(2)}) copy-start(s32[128]{0:T(128)} %param.12) | copy-start | bytes 1540

commit v6 on v5

--- a/solution.py
+++ b/solution.py
@@ -161,6 +161,8 @@
             place = iota((rows, 128), 0) + (at - blk)
             inside = place < length
             if isinstance(at, int) and at >= blk:
+                if at + rows - blk <= frames // 2:
+                    return None
                 return inside
             return (place >= 0) & inside
 
@@ -218,7 +220,10 @@
             kv = kv_ref[pl.ds(at, rows), :]
             kvt_ref[:, pl.ds(at, rows)] = kv.T
             both = mm(kv, wide_rhs)
-            w = jnp.where(usable(at, rows, length), both[:, 0:128], NEG_BIG)
+            w = both[:, 0:128]
+            can = usable(at, rows, length)
+            if can is not None:
+                w = jnp.where(can, w, NEG_BIG)
             ww_ref[pl.ds(at, rows), 0:128] = w
             ww_ref[pl.ds(at, rows), 128:256] = both[:, 128:256]
             return jnp.maximum(top, jnp.max(w, axis=0, keepdims=True))
@@ -263,9 +268,10 @@
             t["near"], t["far"] = mm(kv_ref[t["win"], :], rhs), mm(mkv, rhs)
 
         def softmax(t):
-            s_near = jnp.where(
-                usable(t["at"], 2 * tile, length), t["near"][:, 0:128] + tb_ref[...], NEG_BIG
-            )
+            s_near = t["near"][:, 0:128] + tb_ref[...]
+            can = usable(t["at"], 2 * tile, length)
+            if can is not None:
+                s_near = jnp.where(can, s_near, NEG_BIG)
             s_far = t["far"][:, 0:128]
             high = jnp.maximum(
                 jnp.max(s_near, axis=0, keepdims=True), jnp.max(s_far, axis=0, keepdims=True)
@@ -304,6 +310,9 @@
             y_ref[t["slot"], tile : 2 * tile, :] = jnp.concatenate([d, o], axis=0).astype(BF16).T
 
         stages = (scores, softmax, forward, score_grads, backward, write)
+
+        def settle(slot):
+            y_ref[slot, 0:tile, :] = ww_ref[pl.ds(slot * tile + blk, tile), 0:128].astype(BF16)
 
         def band(first_half, between, i, c):
             tiles = []
@@ -330,7 +339,11 @@
                         ww_ref[pl.ds(t["at"], tile), 0:128] += tail + t["d_near"][0:tile]
                         tail = t["d_near"][tile:]
                         far = far + t["d_far"]
+                        if first_half is None and t["slot"] > slots // 2:
+                            settle(t["slot"] - 1)
             ww_ref[pl.ds(aligned(tiles[-1]["at"] + tile, tile), tile), 0:128] += tail
+            if first_half is None:
+                settle(tiles[-1]["slot"])
             gb_ref[...] = bias
             gm_ref[...] = far
             return c
@@ -380,14 +393,17 @@
                 y_ref[pl.ds(i * GROUP, GROUP), 0:tile, :] = grads.astype(BF16).reshape(
                     GROUP, tile, 128
                 )
-                for u in range(GROUP):
-                    y_ref[i * GROUP + u, 2 * tile :, :] = bias_rows
                 return c
 
             return body
 
         repeat(0, steps // 2, finish(True), 0)
-        repeat(steps // 2, steps, finish(False), 0)
+        if rounds > 1:
+            repeat(steps // 2, steps, finish(False), 0)
+
+        @pl.loop(0, slots, unroll=slots <= 16)
+        def _(slot):
+            y_ref[slot, 2 * tile :, :] = bias_rows
 
 
 def vmem(shape, dtype):

time: 73.2 us -> 73.1 us (level)
  no operation moved by 1% of the time
where the time goes in v6:
time: 73.1 us; the launch traced here: 72.9 us
  blocking collectives  64.3 us (88%)
  Pallas kernels  7.88 us (11%)
    all_to_all x1, blocking collectives, local(): by_frame = lax.all_to_all(grads, 'seq', 0, 0, tiled=True)  32.3 us
    all_to_all x1, blocking collectives, local(): by_head = lax.all_to_all(packed, 'seq', 0, 0, tiled=True)  32 us
    pallas_call x1, Pallas kernels, core_call(): pl.pallas_call(core_kernel, out_shape=jax.ShapeDtypeStruct((slots, 2 * ti...  5.2 us
    pallas_call x1, Pallas kernels, local(): pl.pallas_call(pack_kernel, out_shape=jax.ShapeDtypeStruct((slots, tile,...  1.56 us

profile of v6, /device:TPU:0, one launch (start us, length us, event | category | flops | bytes accessed | tf_op | source)
XLA Modules:
  0.0 72.9 jit_solution(13201194005278744992)
XLA Ops:
  0.6 1.6 %shard_map.110 = bf16[16,128,256]{2,1,0:T(8,128)(2,1)S(1)} custom-call(s32[1,128]{1,0:T(1,128)} %bitcast.3, bf16[128,768]{1,0:T(8,128)(2,1)} %refs_1_.1, bf16[128,768]{1,0:T(8,128)(2,1)} %refs_2_.1, bf16[128,768]{1,0:T(8,128)(2,1)} %refs_3_.1, bf16[128,768]{1,0:T(8,128)(2,1)} %refs_4_.1), custom_call_target="tpu_custom_call" | custom-call | tf_op jit(solution)/shard_map/pallas_call | solution.py:449
  2.2 0.0 copy-start
  2.2 0.0 copy-start.1
  2.2 32.0 %all_to_all.10.x_ref = bf16[16,128,256]{2,1,0:T(8,128)(2,1)S(1)} all-to-all(bf16[16,128,256]{2,1,0:T(8,128)(2,1)S(1)} %shard_map.110), channel_id=1, replica_groups=mesh['groups'=2,'seq'=16] {'seq'}, dimensions={0} | all-to-all | bytes 2097152 | tf_op jit(solution)/shard_map/all_to_all | solution.py:474
  34.3 0.0 copy-done
  34.3 0.0 copy-done.1
  34.3 5.2 %shard_map.111 = bf16[16,264,128]{2,1,0:T(8,128)(2,1)S(1)} custom-call(s32[1,128]{1,0:T(1,128)S(1)} %bitcast.2, f32[12,255]{1,0:T(8,128)S(1)} %copy-done, bf16[16,128,256]{2,1,0:T(8,128)(2,1)S(1)} %all_to_all.10.x_ref), custom_call_target="tpu_custom_call" | custom-call | tf_op jit(solution)/shard_map/pallas_call | solution.py:420
  39.5 32.3 %all_to_all.11.in_ref = bf16[16,264,128]{2,1,0:T(8,128)(2,1)S(1)} all-to-all(bf16[16,264,128]{2,1,0:T(8,128)(2,1)S(1)} %shard_map.111), channel_id=1, replica_groups=mesh['groups'=2,'seq'=16] {'seq'}, dimensions={0} | all-to-all | bytes 2162688 | tf_op jit(solution)/shard_map/all_to_all | solution.py:476
  71.7 1.1 %shard_map.112 = (bf16[128,768]{1,0:T(8,128)(2,1)}, bf16[128,768]{1,0:T(8,128)(2,1)}, bf16[128,768]{1,0:T(8,128)(2,1)}, bf16[128,768]{1,0:T(8,128)(2,1)}, f32[12,255]{1,0:T(8,128)}) custom-call(bf16[16,264,128]{2,1,0:T(8,128)(2,1)S(1)} %all_to_all.11.in_ref), custom_call_target="tpu_custom_call" | custom-call | tf_op jit(solution)/shard_map/pallas_call | solution.py:478
Async XLA Ops:
  2.2 32.1 %copy-start = (f32[12,255]{1,0:T(8,128)S(1)}, f32[12,255]{1,0:T(8,128)}, u32[]{:S(2)}) copy-start(f32[12,255]{1,0:T(8,128)} %bias_ref.1) | copy-start | bytes 36724
  2.2 32.1 %copy-start.1 = (s32[128]{0:T(128)S(1)}, s32[128]{0:T(128)}, u32[]{:S(2)}) copy-start(s32[128]{0:T(128)} %param.12) | copy-start | bytes 1540
